TPU v7x, 32 devices: a whole 2x2x4 slice. The times are simulated.
32 devices in a mesh: members: 2 (over x), row: 16 (over z, y, core).
Axes of the slice: x: 2, y: 2, z: 4, core: 2. Of those that a mesh axis runs over, the one named last changes fastest.
Arguments:
- node_features: bfloat16 [32768, 512], P(('members', 'row')), parts along dimension 0, may hold values from -18 to 18
- nbr_table: int32 [128, 8], P('row'), may hold values from 0 to 27, as said below
- nbr_count: int32 [128], P('row'), may hold values from 4 to 8
- send_block: int32 [256, 1], P('row'), may hold values from 0 to 7
- w_query: bfloat16 [2, 512, 512], replicated, may hold values from -9 to 9
- w_key: bfloat16 [2, 512, 512], replicated, may hold values from -0.7 to 0.7
- w_value: bfloat16 [2, 512, 512], replicated, may hold values from -0.25 to 0.25
- w_out: bfloat16 [2, 512, 512], replicated, may hold values from -0.25 to 0.25
- w_up: bfloat16 [2, 512, 2048], replicated, may hold values from -0.25 to 0.25
- w_down: bfloat16 [2, 2048, 512], replicated, may hold values from -0.125 to 0.125
- w_virtual: bfloat16 [2, 512, 512], replicated, may hold values from -0.25 to 0.25
- gains: float32 [2, 4, 512], replicated, may hold values from 0.25 to 1.75
Outputs:
- latents_out: bfloat16 [32768, 512], P(('members', 'row')), parts along dimension 0
There are 2 independent parts, one for each index of `members`. A program takes and returns all parts, laid end to end along the dimension named above; an argument that names none is the same for every part. Nothing has to cross between parts.
Inputs may be any that keep to these rules, and one draw needn't show every extreme that they name: `nbr_table`: The first entry of each row is the block itself. Every live entry names a block that exists.
All inputs are finite; a program needn't handle non-finite values.
Results may differ from a plain program's by a relative error of at most 0.007.
Values may be sent and summed in bfloat16 or wider, within the bound.
A program may use at most 128 MiB of HBM per device.

v0:
```python
import functools
import math

import jax
import jax.numpy as jnp
from jax import lax
from jax.experimental import pallas as pl
from jax.experimental.pallas import tpu as pltpu
from jax.sharding import PartitionSpec as P

HEADS = 4
HALO_B = 2
TAIL = 16
VMEM_LIMIT = 60 * 1024 * 1024


def normalize(values, scaling):
    centred = values - jnp.mean(values, axis=-1, keepdims=True)
    spread = jnp.mean(centred * centred, axis=-1, keepdims=True)
    return centred * lax.rsqrt(spread + 1e-05) * scaling


def dot(a, b):
    return jnp.dot(a, b, preferred_element_type=jnp.float32)


def gelu(x):
    return 0.5 * x * (1.0 + jnp.tanh(math.sqrt(2 / math.pi) * (x + 0.044715 * x * x * x)))


def fill_send(send_sm, normed_ref, total, send_ref, block):
    peers, slots = send_sm.shape
    width = normed_ref.shape[1]
    high = total.astype(jnp.bfloat16).astype(jnp.float32)
    line = lax.broadcasted_iota(jnp.int32, (TAIL, width), 0)
    tail = jnp.where(line == 0, high, jnp.where(line == 1, total - high, 0.0)).astype(jnp.bfloat16)

    def one(peer, carry):
        for slot in range(slots):
            own = pl.multiple_of(send_sm[peer, slot] * block, block)
            send_ref[peer, pl.ds(slot * block, block), :] = normed_ref[pl.ds(own, block), :]
        send_ref[peer, pl.ds(slots * block, TAIL), :] = tail
        return carry

    lax.fori_loop(0, peers, one, 0)


def first_kernel(block, rows, send_sm, x_ref, gains_ref, normed_ref, send_ref):
    total = jnp.zeros((1, x_ref.shape[1]), jnp.float32)
    for start in range(0, x_ref.shape[0], rows):
        x = x_ref[pl.ds(start, rows), :].astype(jnp.float32)
        total = total + jnp.sum(x, axis=0, keepdims=True)
        normed_ref[pl.ds(start, rows), :] = normalize(x, gains_ref[0, 0:1, :]).astype(jnp.bfloat16)
    fill_send(send_sm, normed_ref, total, send_ref, block)


def layer_kernel(layer, last, block, node_total, *refs):
    (table_sm, count_sm, send_sm, x_ref, normed_ref, low_ref, high_ref, far_ref, wq_ref, wk_ref, wv_ref,
     wo_ref, wu_ref, wd_ref, wm_ref, gains_ref) = refs[:16]
    if last:
        out_ref, key_ref, value_ref, context_ref, virtual_ref = refs[16:]
    else:
        out_ref, next_ref, send_ref, key_ref, value_ref, context_ref, virtual_ref, sum_ref = refs[16:]
    step = pl.program_id(0)
    rows, width = x_ref.shape
    blocks_here, slots_listed = table_sm.shape
    peers = far_ref.shape[0]
    slots = (far_ref.shape[1] - TAIL) // block
    head_size = width // HEADS
    group = rows // block
    base = low_ref.shape[0]
    own_rows = normed_ref.shape[0]

    @pl.when(step == 0)
    def _():
        def project(piece, at):
            size = piece.shape[0]
            key_ref[pl.ds(at, size), :] = dot(piece, wk_ref[...]).astype(jnp.bfloat16)
            value_ref[pl.ds(at, size), :] = dot(piece, wv_ref[...]).astype(jnp.bfloat16)

        project(low_ref[...], 0)
        project(high_ref[...], base + own_rows)
        chunk = math.gcd(own_rows, 512)

        def own_piece(i, carry):
            at = pl.multiple_of(i * chunk, chunk)
            project(normed_ref[pl.ds(at, chunk), :], pl.multiple_of(base + at, block))
            return carry

        lax.fori_loop(0, own_rows // chunk, own_piece, 0)
        many = math.gcd(peers, 4)
        span = slots * block

        def far_piece(i, carry):
            piece = far_ref[pl.ds(i * many, many), pl.ds(0, span), :].reshape(many * span, width)
            project(piece, pl.multiple_of(2 * base + own_rows + i * (many * span), block))
            return carry

        lax.fori_loop(0, peers // many, far_piece, 0)
        tails = far_ref[:, pl.ds(span, TAIL), :].astype(jnp.float32)
        node_sum = jnp.sum(jnp.sum(tails, axis=0), axis=0, keepdims=True)
        mean = jnp.broadcast_to(node_sum / node_total, (TAIL, width)).astype(jnp.bfloat16)
        virtual_ref[...] = dot(mean, wm_ref[...])

    at = pl.multiple_of(step * rows, rows)
    queries = dot(normed_ref[pl.ds(at, rows), :], wq_ref[...]).astype(jnp.bfloat16)
    scale = math.log2(math.e) / math.sqrt(head_size)
    for g in range(group):
        which = step * group + g
        count = count_sm[which]
        places = [pl.multiple_of(table_sm[which, j] * block, block) for j in range(slots_listed)]
        for h in range(HEADS):
            columns = slice(h * head_size, (h + 1) * head_size)
            q = queries[g * block : (g + 1) * block, columns]
            scores = []
            for j in range(slots_listed):
                k = key_ref[pl.ds(places[j], block), columns]
                s = lax.dot_general(q, k, (((1,), (1,)), ((), ())), preferred_element_type=jnp.float32)
                scores.append(s if j == 0 else jnp.where(j < count, s, -1e30))
            top = jnp.max(functools.reduce(jnp.maximum, scores), axis=-1, keepdims=True)
            weights = [jnp.exp2((s - top) * scale) for s in scores]
            norm = jnp.sum(functools.reduce(jnp.add, weights), axis=-1, keepdims=True)
            probs = jnp.concatenate([w.astype(jnp.bfloat16) for w in weights], axis=1)
            v = jnp.concatenate([value_ref[pl.ds(p, block), columns] for p in places], axis=0)
            context_ref[pl.ds(g * block, block), columns] = (dot(probs, v) / norm).astype(jnp.bfloat16)

    x = x_ref[...].astype(jnp.float32)
    after_att = x + normalize(dot(context_ref[...], wo_ref[...]), gains_ref[layer, 1:2, :])
    middle = normalize(after_att, gains_ref[layer, 2:3, :]).astype(jnp.bfloat16)
    hidden_size = wu_ref.shape[1]
    part = math.gcd(hidden_size, 512)
    down = None
    for f in range(0, hidden_size, part):
        hidden = gelu(dot(middle, wu_ref[:, f : f + part])).astype(jnp.bfloat16)
        term = dot(hidden, wd_ref[f : f + part, :])
        down = term if down is None else down + term
    output_part = normalize(down, gains_ref[layer, 3:4, :])
    latent = (after_att + output_part + virtual_ref[0:1, :]).astype(jnp.bfloat16)
    out_ref[...] = latent
    if not last:
        current = latent.astype(jnp.float32)
        next_ref[pl.ds(at, rows), :] = normalize(current, gains_ref[layer + 1, 0:1, :]).astype(jnp.bfloat16)
        partial = jnp.sum(current, axis=0, keepdims=True)

        @pl.when(step == 0)
        def _():
            sum_ref[0:1, :] = partial

        @pl.when(step > 0)
        def _():
            sum_ref[0:1, :] = sum_ref[0:1, :] + partial

        @pl.when(step == pl.num_programs(0) - 1)
        def _():
            fill_send(send_sm, next_ref, sum_ref[0:1, :], send_ref, block)


def fixed(shape):
    return pl.BlockSpec(shape, lambda i, *_: (0,) * len(shape), pipeline_mode=pl.Buffered(1))


def body(
    node_features,
    nbr_table,
    nbr_count,
    send_block,
    w_query,
    w_key,
    w_value,
    w_out,
    w_up,
    w_down,
    w_virtual,
    gains,
):
    blocks_here = nbr_table.shape[0]
    own_rows, width = node_features.shape
    block = own_rows // blocks_here
    peers = lax.axis_size("row")
    slots = send_block.shape[1]
    layers = w_query.shape[0]
    rows = block * math.gcd(blocks_here, 2)
    sent = jax.ShapeDtypeStruct((peers, slots * block + TAIL, width), jnp.bfloat16)
    held = jax.ShapeDtypeStruct((own_rows, width), jnp.bfloat16)
    halo = HALO_B * block
    params = pltpu.CompilerParams(vmem_limit_bytes=VMEM_LIMIT)

    normed, send = pl.pallas_call(
        functools.partial(first_kernel, block, rows),
        out_shape=(held, sent),
        grid_spec=pltpu.PrefetchScalarGridSpec(
            num_scalar_prefetch=1,
            grid=(1,),
            in_specs=[fixed(held.shape), fixed(gains.shape)],
            out_specs=[fixed(held.shape), fixed(sent.shape)],
        ),
        compiler_params=params,
        name="first",
    )(send_block, node_features, gains)

    latent = node_features
    for layer in range(layers):
        last = layer == layers - 1
        far = lax.all_to_all(send, "row", split_axis=0, concat_axis=0, tiled=True)
        low = lax.ppermute(normed[own_rows - halo :], "row", [(i, i + 1) for i in range(peers - 1)])
        high = lax.ppermute(normed[:halo], "row", [(i + 1, i) for i in range(peers - 1)])

        def of_layer(w, layer=layer):
            return pl.BlockSpec(
                (None,) + w.shape[1:], lambda i, *_: (layer, 0, 0), pipeline_mode=pl.Buffered(1)
            )

        tile = pl.BlockSpec((rows, width), lambda i, *_: (i, 0))
        table_rows = 2 * halo + own_rows + peers * slots * block
        weights = (w_query, w_key, w_value, w_out, w_up, w_down, w_virtual)
        scratch = [
            pltpu.VMEM((table_rows, width), jnp.bfloat16),
            pltpu.VMEM((table_rows, width), jnp.bfloat16),
            pltpu.VMEM((rows, width), jnp.bfloat16),
            pltpu.VMEM((TAIL, width), jnp.float32),
        ]
        result = pl.pallas_call(
            functools.partial(layer_kernel, layer, last, block, own_rows * peers),
            out_shape=(held,) if last else (held, held, sent),
            grid_spec=pltpu.PrefetchScalarGridSpec(
                num_scalar_prefetch=3,
                grid=(own_rows // rows,),
                in_specs=[tile, fixed(held.shape), fixed(low.shape), fixed(high.shape), fixed(far.shape)]
                + [of_layer(w) for w in weights]
                + [fixed(gains.shape)],
                out_specs=[tile] if last else [tile, fixed(held.shape), fixed(sent.shape)],
                scratch_shapes=scratch if last else scratch + [pltpu.VMEM((8, width), jnp.float32)],
            ),
            compiler_params=params,
            name=f"layer{layer}",
        )(nbr_table, nbr_count, send_block, latent, normed, low, high, far, *weights, gains)
        if last:
            (latent,) = result
        else:
            latent, normed, send = result
    return latent


def solution(mesh):
    in_specs = (
        P(("members", "row"), None),
        P("row", None),
        P("row"),
        P("row", None),
        P(),
        P(),
        P(),
        P(),
        P(),
        P(),
        P(),
        P(),
    )
    out_specs = P(("members", "row"), None)
    return jax.shard_map(body, mesh=mesh, in_specs=in_specs, out_specs=out_specs, check_vma=False)
```

profile of v0, /device:TPU:15, one launch (start us, length us, event | category | flops | bytes accessed | tf_op | source)
XLA Modules:
  0.0 207.7 jit_solution(10568795032285340385)
XLA Ops:
  0.0 1.3 copy.15.send_sm.refs_2_
  1.3 4.7 %first.1 = (bf16[1024,512]{1,0:T(8,128)(2,1)}, bf16[16,144,512]{2,1,0:T(8,128)(2,1)}) custom-call(s32[16,1]{1,0:T(8,128)} %copy.15.send_sm.refs_2_, bf16[1024,512]{1,0:T(8,128)(2,1)} %refs_3_.1, f32[2,4,512]{2,1,0:T(4,128)} %refs_15_.3), custom_call_target="tpu_custom_call" | custom-call | tf_op jit(solution)/shard_map/first/pallas_call | solution.py:188
  6.0 0.0 copy-start.3
  6.0 6.7 %all-to-all-start = ((bf16[16,144,512]{2,1,0:T(8,128)(2,1)}), bf16[16,144,512]{2,1,0:T(8,128)(2,1)S(1)}, u32[]{:S(2)}, u32[]{:S(2)}) async-start(bf16[16,144,512]{2,1,0:T(8,128)(2,1)} %get-tuple-element.11), calls=%async_computation | async-start | bytes 4718592 | tf_op jit(solution)/shard_map/all_to_all | solution.py:204
  12.7 0.0 copy-done.3
  12.7 2.3 %collective-permute-start.1 = (bf16[256,512]{1,0:T(8,128)(2,1)S(1)}, bf16[256,512]{1,0:T(8,128)(2,1)S(1)}, u32[]{:S(2)}, u32[]{:S(2)}) collective-permute-start(bf16[256,512]{1,0:T(8,128)(2,1)S(1)} %get-tuple-element.17), channel_id=1, source_target_pairs={{1,0},{2,1},{3,2},{4,3},{5,4},{6,5},{7,6},{8,7},{9,8},{10,9},{11,1... | collective-permute-start | bytes 786440 | tf_op jit(solution)/shard_map/ppermute | solution.py:206
  15.0 4.2 %collective-permute-start = (bf16[256,512]{1,0:T(8,128)(2,1)S(1)}, bf16[256,512]{1,0:T(8,128)(2,1)S(1)}, u32[]{:S(2)}, u32[]{:S(2)}) collective-permute-start(bf16[256,512]{1,0:T(8,128)(2,1)S(1)} %get-tuple-element.18), channel_id=1, source_target_pairs={{0,1},{1,2},{2,3},{3,4},{4,5},{5,6},{6,7},{7,8},{8,9},{9,10},{10,1... | collective-permute-start | bytes 786440 | tf_op jit(solution)/shard_map/ppermute | solution.py:205
  19.2 49.3 %collective-permute-done.1.refs_6_ = bf16[256,512]{1,0:T(8,128)(2,1)S(1)} collective-permute-done((bf16[256,512]{1,0:T(8,128)(2,1)S(1)}, bf16[256,512]{1,0:T(8,128)(2,1)S(1)}, u32[]{:S(2)}, u32[]{:S(2)}) %collective-permute-start.1) | collective-permute-done | bytes 262176 | tf_op jit(solution)/shard_map/ppermute | solution.py:206
  68.5 0.0 copy-start.4
  68.5 0.0 collective-permute-done.refs_5_
  68.5 0.0 copy-start.6
  68.5 0.0 all-to-all-done.refs_7_
  68.5 0.7 copy-done.4
  69.2 0.1 copy-done.6
  69.3 0.0 copy-start
  69.3 1.4 copy-done
  70.7 38.6 %layer0.1 = (bf16[1024,512]{1,0:T(8,128)(2,1)}, bf16[1024,512]{1,0:T(8,128)(2,1)}, bf16[16,144,512]{2,1,0:T(8,128)(2,1)}) custom-call(s32[8,8]{1,0:T(8,128)} %refs_0_.3, s32[8]{0:T(128)} %refs_1_.3, s32[16,1]{1,0:T(8,128)} %copy.15.send_sm.refs_2_, bf16[1024,512]{1,0:T(8,128)(2,1)} %refs_3_.1, bf16[1024,512]{1,0:T(8,128)(2,1)} %get-tuple-element.10.refs_4_, ...), custom_call_target="tpu_custom_call" | custom-call | tf_op jit(solution)/shard_map/layer0/pallas_call | solution.py:222
  109.4 0.0 copy-start.2
  109.4 4.5 %all-to-all-start.1 = ((bf16[16,144,512]{2,1,0:T(8,128)(2,1)}), bf16[16,144,512]{2,1,0:T(8,128)(2,1)S(1)}, u32[]{:S(2)}, u32[]{:S(2)}) async-start(bf16[16,144,512]{2,1,0:T(8,128)(2,1)} %get-tuple-element.14), calls=%async_computation.1 | async-start | bytes 4718592 | tf_op jit(solution)/shard_map/all_to_all | solution.py:204
  113.9 0.0 copy-done.2
  113.9 2.3 %collective-permute-start.3 = (bf16[256,512]{1,0:T(8,128)(2,1)S(1)}, bf16[256,512]{1,0:T(8,128)(2,1)S(1)}, u32[]{:S(2)}, u32[]{:S(2)}) collective-permute-start(bf16[256,512]{1,0:T(8,128)(2,1)S(1)} %get-tuple-element.15), channel_id=1, source_target_pairs={{1,0},{2,1},{3,2},{4,3},{5,4},{6,5},{7,6},{8,7},{9,8},{10,9},{11,1... | collective-permute-start | bytes 786440 | tf_op jit(solution)/shard_map/ppermute | solution.py:206
  116.2 4.3 %collective-permute-start.2 = (bf16[256,512]{1,0:T(8,128)(2,1)S(1)}, bf16[256,512]{1,0:T(8,128)(2,1)S(1)}, u32[]{:S(2)}, u32[]{:S(2)}) collective-permute-start(bf16[256,512]{1,0:T(8,128)(2,1)S(1)} %get-tuple-element.16), channel_id=1, source_target_pairs={{0,1},{1,2},{2,3},{3,4},{4,5},{5,6},{6,7},{7,8},{8,9},{9,10},{10,1... | collective-permute-start | bytes 786440 | tf_op jit(solution)/shard_map/ppermute | solution.py:205
  120.6 49.1 %collective-permute-done.3.refs_6_ = bf16[256,512]{1,0:T(8,128)(2,1)S(1)} collective-permute-done((bf16[256,512]{1,0:T(8,128)(2,1)S(1)}, bf16[256,512]{1,0:T(8,128)(2,1)S(1)}, u32[]{:S(2)}, u32[]{:S(2)}) %collective-permute-start.3) | collective-permute-done | bytes 262176 | tf_op jit(solution)/shard_map/ppermute | solution.py:206
  169.7 0.0 copy-start.5
  169.7 0.0 collective-permute-done.2.refs_5_
  169.7 0.0 copy-start.7
  169.7 0.0 all-to-all-done.1.refs_7_
  169.7 0.0 copy-start.1
  169.7 0.7 copy-done.5
  170.4 0.1 copy-done.7
  170.5 0.8 copy-done.1
  171.3 36.4 %layer1.1 = bf16[1024,512]{1,0:T(8,128)(2,1)} custom-call(s32[8,8]{1,0:T(8,128)} %refs_0_.3, s32[8]{0:T(128)} %refs_1_.3, s32[16,1]{1,0:T(8,128)} %copy.15.send_sm.refs_2_, bf16[1024,512]{1,0:T(8,128)(2,1)} %get-tuple-element.12.refs_3_, bf16[1024,512]{1,0:T(8,128)(2,1)} %get-tuple-element.13.refs_4_, bf16[256,512]{1,0:T(8,128)(2,1)} %copy-done.7, ...), custom_call_target="tpu_custom_call" | custom-call | tf_op jit(solution)/shard_map/layer1/pallas_call | solution.py:222
  (2 shorter events, 0.1 us)
Async XLA Ops:
  6.0 6.7 %copy-start.3 = (bf16[1024,512]{1,0:T(8,128)(2,1)S(1)}, bf16[1024,512]{1,0:T(8,128)(2,1)}, u32[]{:S(2)}) copy-start(bf16[1024,512]{1,0:T(8,128)(2,1)} %get-tuple-element.10.refs_4_) | copy-start | bytes 3145732
  6.0 62.5 %all-to-all-start = ((bf16[16,144,512]{2,1,0:T(8,128)(2,1)}), bf16[16,144,512]{2,1,0:T(8,128)(2,1)S(1)}, u32[]{:S(2)}, u32[]{:S(2)}) async-start(bf16[16,144,512]{2,1,0:T(8,128)(2,1)} %get-tuple-element.11), calls=%async_computation | async-start | bytes 4718592 | tf_op jit(solution)/shard_map/all_to_all | solution.py:204
  12.7 55.8 %collective-permute-start.1 = (bf16[256,512]{1,0:T(8,128)(2,1)S(1)}, bf16[256,512]{1,0:T(8,128)(2,1)S(1)}, u32[]{:S(2)}, u32[]{:S(2)}) collective-permute-start(bf16[256,512]{1,0:T(8,128)(2,1)S(1)} %get-tuple-element.17), channel_id=1, source_target_pairs={{1,0},{2,1},{3,2},{4,3},{5,4},{6,5},{7,6},{8,7},{9,8},{10,9},{11,1... | collective-permute-start | bytes 786440 | tf_op jit(solution)/shard_map/ppermute | solution.py:206
  15.0 53.5 %collective-permute-start = (bf16[256,512]{1,0:T(8,128)(2,1)S(1)}, bf16[256,512]{1,0:T(8,128)(2,1)S(1)}, u32[]{:S(2)}, u32[]{:S(2)}) collective-permute-start(bf16[256,512]{1,0:T(8,128)(2,1)S(1)} %get-tuple-element.18), channel_id=1, source_target_pairs={{0,1},{1,2},{2,3},{3,4},{4,5},{5,6},{6,7},{7,8},{8,9},{9,10},{10,1... | collective-permute-start | bytes 786440 | tf_op jit(solution)/shard_map/ppermute | solution.py:205
  68.5 0.7 copy-start.4
  68.5 0.8 copy-start.6
  69.3 1.4 copy-start
  109.4 4.5 %copy-start.2 = (bf16[1024,512]{1,0:T(8,128)(2,1)S(1)}, bf16[1024,512]{1,0:T(8,128)(2,1)}, u32[]{:S(2)}) copy-start(bf16[1024,512]{1,0:T(8,128)(2,1)} %get-tuple-element.13.refs_4_) | copy-start | bytes 3145732
  109.4 60.3 %all-to-all-start.1 = ((bf16[16,144,512]{2,1,0:T(8,128)(2,1)}), bf16[16,144,512]{2,1,0:T(8,128)(2,1)S(1)}, u32[]{:S(2)}, u32[]{:S(2)}) async-start(bf16[16,144,512]{2,1,0:T(8,128)(2,1)} %get-tuple-element.14), calls=%async_computation.1 | async-start | bytes 4718592 | tf_op jit(solution)/shard_map/all_to_all | solution.py:204
  113.9 55.8 %collective-permute-start.3 = (bf16[256,512]{1,0:T(8,128)(2,1)S(1)}, bf16[256,512]{1,0:T(8,128)(2,1)S(1)}, u32[]{:S(2)}, u32[]{:S(2)}) collective-permute-start(bf16[256,512]{1,0:T(8,128)(2,1)S(1)} %get-tuple-element.15), channel_id=1, source_target_pairs={{1,0},{2,1},{3,2},{4,3},{5,4},{6,5},{7,6},{8,7},{9,8},{10,9},{11,1... | collective-permute-start | bytes 786440 | tf_op jit(solution)/shard_map/ppermute | solution.py:206
  116.2 53.5 %collective-permute-start.2 = (bf16[256,512]{1,0:T(8,128)(2,1)S(1)}, bf16[256,512]{1,0:T(8,128)(2,1)S(1)}, u32[]{:S(2)}, u32[]{:S(2)}) collective-permute-start(bf16[256,512]{1,0:T(8,128)(2,1)S(1)} %get-tuple-element.16), channel_id=1, source_target_pairs={{0,1},{1,2},{2,3},{3,4},{4,5},{5,6},{6,7},{7,8},{8,9},{9,10},{10,1... | collective-permute-start | bytes 786440 | tf_op jit(solution)/shard_map/ppermute | solution.py:205
  169.7 0.7 copy-start.5
  169.7 0.8 copy-start.7
  169.7 1.6 copy-start.1
where the time goes:
time: 208 us
  waiting for transfers between devices  98.5 us (47%)
  Pallas kernels  79.7 us (38%)
  starting transfers between devices  24.2 us (12%)
  local copies, waits for them, and re-layouts  5.19 us (2%)
    ppermute x2, waiting for transfers between devices, body(): lax.ppermute(normed[:halo], 'row', [(i + 1, i) for i in range(peers - 1)])  98.5 us
    pallas_call x2, Pallas kernels, body(): pl.pallas_call(functools.partial(layer_kernel, layer, last, block, own_ro...  75 us
    all_to_all x2, starting transfers between devices, body(): far = lax.all_to_all(send, 'row', split_axis=0, concat_axis=0, tiled=True)  11.1 us
    ppermute x2, starting transfers between devices, body(): lax.ppermute(normed[own_rows - halo:], 'row', [(i, i + 1) for i in range(...  8.5 us
    unnamed x17, local copies, waits for them, and re-layouts  5.11 us
    pallas_call x1, Pallas kernels, body(): pl.pallas_call(functools.partial(first_kernel, block, rows), out_shape=(h...  4.67 us
    ppermute x2, starting transfers between devices, body(): lax.ppermute(normed[:halo], 'row', [(i + 1, i) for i in range(peers - 1)])  4.61 us
  transfers between devices with their start and end apart: 6, of which 2 were waited for; matrix products, arithmetic and copies ran while one was open for 0% of the time, Pallas kernels for 0%

commit v1 on v0

v1 whole, which is shorter than its diff:
```python
import functools
import math

import jax
import jax.numpy as jnp
from jax import lax
from jax.experimental import pallas as pl
from jax.experimental.pallas import tpu as pltpu
from jax.sharding import PartitionSpec as P

HEADS = 4
HALO_B = 2
VMEM_LIMIT = 67_000_000
MESH = pl.DeviceIdType.MESH
BF16 = jnp.bfloat16
F32 = jnp.float32
AXIS = "row"


def normalize(values, scaling):
    centred = values - jnp.mean(values, axis=-1, keepdims=True)
    spread = jnp.mean(centred * centred, axis=-1, keepdims=True)
    return centred * lax.rsqrt(spread + 1e-05) * scaling


def dot(a, b, contract=((1,), (0,))):
    return lax.dot_general(a, b, (contract, ((), ())), preferred_element_type=F32)


def gelu(x):
    return 0.5 * x * (1.0 + jnp.tanh(math.sqrt(2 / math.pi) * (x + 0.044715 * x * x * x)))


def flip(a, b, bits):
    out = 0
    for bit in range(bits):
        weight = 1 << bit
        x = lax.rem(lax.div(a, jnp.int32(weight)), jnp.int32(2))
        y = lax.rem(lax.div(b, jnp.int32(weight)), jnp.int32(2))
        out = out + weight * lax.rem(x + y, jnp.int32(2))
    return out


def below(a, b):
    return jnp.minimum(jnp.maximum(b - a, 0), 1)


def equal(a, b):
    return 1 - jnp.minimum(jnp.maximum(a - b, b - a), 1)


def kernel(shapes, table_sm, count_sm, send_sm, x_ref, gains_ref, wq_hbm, wk_hbm, wv_hbm, wo_hbm, wu_hbm, wd_hbm,
           wm_hbm, out_ref, wq, wk, wv, wo, wu, wd, wm, normed, latent, keys, values, context, send_buf, far,
           halo_send, halo, sum_send, sums, total_ref, virtual, perm_sm, pos_sm, place_sm, w_sem, far_send, far_recv,
           halo_ssem, halo_rsem, sum_ssem, sum_rsem):
    peers, layers, blocks, block, width, slots, listed, group, node_total = shapes
    near = 2 * HALO_B + blocks
    bits = peers.bit_length() - 1
    half, quarter = peers // 2, peers // 4
    rows = group * block
    steps = blocks // group
    head = width // HEADS
    hidden_size = wu.shape[-1]
    me = lax.axis_index(AXIS)
    inner = jnp.where((me >= quarter) & (me < half + quarter), 1, 0)

    def order(layer, k):
        outer = jnp.where(k < half, half + k, peers - 1 - k)
        if layer == 0:
            inside = jnp.where(k < half - 1, half - 1 - k, peers - 1 - (k - (half - 1)))
        else:
            late = k - quarter
            inside = jnp.where(
                late < 0, peers - 1 - k, jnp.where(late < half - 1, half - 1 - late, peers - 1 - quarter - (late - half + 1))
            )
        return flip(me, jnp.where(inner == 1, inside, outer), bits)

    def remote(src, dst, ssem, rsem, to):
        return pltpu.make_async_remote_copy(
            src_ref=src, dst_ref=dst, send_sem=ssem, recv_sem=rsem, device_id={AXIS: to}, device_id_type=MESH
        )

    def far_out(layer, to):
        return remote(send_buf.at[layer, to], far.at[layer, me], far_send.at[layer, to], far_recv.at[layer, me], to)

    def far_in(layer, source):
        return remote(
            send_buf.at[layer, source], far.at[layer, source], far_send.at[layer, source], far_recv.at[layer, source], source
        )

    def sum_out(layer, to):
        return remote(sum_send.at[layer], sums.at[layer, me], sum_ssem.at[layer, to], sum_rsem.at[layer, me], to)

    def sum_in(layer, source):
        return remote(sum_send.at[layer], sums.at[layer, source], sum_ssem.at[layer, source], sum_rsem.at[layer, source], source)

    def halo_copy(layer, side, to):
        return remote(
            halo_send.at[layer, side], halo.at[layer, 1 - side], halo_ssem.at[layer, side], halo_rsem.at[layer, 1 - side], to
        )

    def halo_each(layer, act):
        @pl.when(me > 0)
        def _():
            act(halo_copy(layer, 0, me - 1), 0)

        @pl.when(me < peers - 1)
        def _():
            act(halo_copy(layer, 1, me + 1), 1)

    barrier = pltpu.get_barrier_semaphore()

    def greet(k, carry):
        pl.semaphore_signal(barrier, inc=1, device_id={AXIS: lax.rem(me + k, peers)}, device_id_type=MESH)
        return carry

    lax.fori_loop(1, peers, greet, 0)

    loads = []
    for layer in range(layers):
        for n, (src, dst) in enumerate(
            ((wk_hbm, wk), (wv_hbm, wv), (wm_hbm, wm), (wq_hbm, wq), (wo_hbm, wo), (wu_hbm, wu), (wd_hbm, wd))
        ):
            loads.append(pltpu.make_async_copy(src.at[layer], dst.at[layer], w_sem.at[layer, n]))
    for load in loads:
        load.start()

    total_ref[0:1, :] = jnp.zeros((1, width), F32)

    def first(i, carry):
        x = x_ref[pl.ds(i * group, group)].reshape(rows, width).astype(F32)
        total_ref[0:1, :] = total_ref[0:1, :] + jnp.sum(x, axis=0, keepdims=True)
        fresh = normalize(x, gains_ref[0, 0:1, :]).astype(BF16)
        normed[0, pl.ds(i * group, group)] = fresh.reshape(group, block, width)
        return carry

    lax.fori_loop(0, steps, first, 0)

    def stage(layer, to):
        for slot in range(slots):
            at = send_sm[to * slots + slot]
            if layer > 0:
                at = pos_sm[at]
            send_buf[layer, to, pl.ds(slot * block, block), :] = normed[layer, at]

    def stage_self(layer):
        for slot in range(slots):
            at = send_sm[me * slots + slot]
            if layer > 0:
                at = pos_sm[at]
            far[layer, me, pl.ds(slot * block, block), :] = normed[layer, at]

    def stage_edges(layer):
        for side in range(2):
            for b in range(HALO_B):
                at = b if side == 0 else blocks - HALO_B + b
                if layer > 0:
                    at = pos_sm[at]
                halo_send[layer, side, pl.ds(b * block, block), :] = normed[layer, at]
        for k in range(width // 128):
            part = total_ref[0:1, k * 128 : (k + 1) * 128]
            sum_send[layer, k : k + 1, :] = part
            sums[layer, me, k : k + 1, :] = part

    def send_edges(layer):
        def one(k, carry):
            sum_out(layer, order(layer, k)).start()
            return carry

        lax.fori_loop(0, peers - 1, one, 0)
        halo_each(layer, lambda copy, side: copy.start())

    def stage_all(k, carry):
        stage(0, order(0, k))
        return carry

    def send_all(k, carry):
        far_out(0, order(0, k)).start()
        return carry

    stage_edges(0)
    lax.fori_loop(0, peers - 1, stage_all, 0)
    pl.semaphore_wait(barrier, peers - 1)
    send_edges(0)
    lax.fori_loop(0, peers - 1, send_all, 0)
    stage_self(0)

    uses = [jnp.int32(peers * slots + n) for n in range(blocks)]
    for k in range(peers - 2, -1, -1):
        to = order(1, jnp.int32(k))
        for slot in range(slots - 1, -1, -1):
            b = send_sm[to * slots + slot]
            uses = [use + equal(b, n) * (k * slots + slot - use) for n, use in enumerate(uses)]
    places = []
    for n in range(blocks):
        place = jnp.int32(0)
        for other in range(blocks):
            if other != n:
                place = place + below(uses[other], uses[n])
        places.append(place)
        pos_sm[n] = place
    for n in range(blocks):
        which = jnp.int32(0)
        for b in range(blocks):
            which = which + equal(places[b], n) * b
        perm_sm[n] = which
    for t in range(near + peers * slots):
        place_sm[0, t] = jnp.int32(t)
        own_b = t - HALO_B
        place_sm[1, t] = HALO_B + places[own_b] if 0 <= own_b < blocks else jnp.int32(t)

    count_w = 7

    def use(layer, names):
        for n in names:
            loads[layer * count_w + n].wait()

    def project(layer, piece, at):
        count = piece.shape[0]
        flat = piece.reshape(count * block, width)
        keys[pl.ds(at, count)] = dot(flat, wk[layer]).astype(BF16).reshape(count, block, width)
        turned = dot(wv[layer], flat, ((0,), (1,))).astype(BF16)
        for n in range(count):
            values[at + n] = turned[:, n * block : (n + 1) * block]

    def gather(layer):
        chunk = math.gcd(blocks, 4)

        def own_piece(i, carry):
            project(layer, normed[layer, pl.ds(i * chunk, chunk)], HALO_B + i * chunk)
            return carry

        lax.fori_loop(0, blocks // chunk, own_piece, 0)

        def halo_in(copy, side):
            copy.wait_recv()
            project(layer, halo[layer, side].reshape(HALO_B, block, width), 0 if side == 0 else HALO_B + blocks)

        @pl.when(me > 0)
        def _():
            halo_in(halo_copy(layer, 1, me - 1), 0)

        @pl.when(me < peers - 1)
        def _():
            halo_in(halo_copy(layer, 0, me + 1), 1)

        many = math.gcd(quarter, 4)
        for inside, outside in ((2, 0), (0, 1), (1, 3), (3, 2)):
            part = flip(lax.div(me, jnp.int32(quarter)), jnp.where(inner == 1, inside, outside), 2) * quarter

            def wait_one(n, carry, part=part):
                source = part + n

                @pl.when(source != me)
                def _():
                    far_in(layer, source).wait_recv()

                return carry

            def far_piece(i, carry, part=part):
                source = part + i * many
                lax.fori_loop(i * many, (i + 1) * many, wait_one, 0)
                piece = far[layer, pl.ds(source, many)].reshape(many * slots, block, width)
                project(layer, piece, near + source * slots)
                return carry

            lax.fori_loop(0, quarter // many, far_piece, 0)

        def sum_wait(k, carry):
            sum_in(layer, order(layer, k)).wait_recv()
            return carry

        lax.fori_loop(0, peers - 1, sum_wait, 0)
        whole = jnp.sum(sums[layer], axis=0)
        mean = jnp.concatenate([whole[k : k + 1, :] for k in range(width // 128)], axis=1) / node_total
        mean = jnp.broadcast_to(mean, (16, width)).astype(BF16)
        virtual[...] = dot(mean, wm[layer])

    scale = math.log2(math.e) / math.sqrt(head)

    def attend(layer, which, queries, at):
        count = count_sm[which]
        home = table_sm[which, 0]
        spots = []
        for j in range(listed):
            entry = table_sm[which, j]
            if 2 * j >= listed:
                entry = home + below(j, count) * (entry - home)
            spots.append(place_sm[layer, entry])
        dead = [(1 - below(j, count)).astype(F32) * -1e30 for j in range(listed)]
        blank = jnp.zeros((head, block), BF16)
        for h in range(0, HEADS, 2):
            pair = slice(h * head, (h + 2) * head)
            upper = queries[h * head : (h + 1) * head, at : at + block]
            lower = queries[(h + 1) * head : (h + 2) * head, at : at + block]
            both = jnp.concatenate(
                [jnp.concatenate([upper, blank], axis=1), jnp.concatenate([blank, lower], axis=1)], axis=0
            )
            scores = []
            for j in range(listed):
                s = dot(keys[spots[j], :, pair], both)
                scores.append(s if 2 * j < listed else s + dead[j])
            top = jnp.max(functools.reduce(jnp.maximum, scores), axis=0, keepdims=True)
            weights = [jnp.exp2((s - top) * scale) for s in scores]
            inverse = 1.0 / jnp.sum(functools.reduce(jnp.add, weights), axis=0, keepdims=True)
            probs = jnp.concatenate([w.astype(BF16) for w in weights], axis=0)
            v = jnp.concatenate([values[p, pair] for p in spots], axis=1)
            mixed = dot(v, probs)
            for n in range(2):
                part = slice(n * block, (n + 1) * block)
                of_head = slice((h + n) * head, (h + n + 1) * head)
                context[of_head, at : at + block] = (
                    mixed[n * head : (n + 1) * head, part] * inverse[:, part]
                ).astype(BF16)

    def block_step(layer, i):
        last = layer == layers - 1
        order_at = [i * group + g for g in range(group)]
        if last:
            which = order_at
            source = [pos_sm[w] for w in which]
        else:
            which = [perm_sm[n] for n in order_at]
            source = which
        mine = jnp.concatenate([normed[layer, s] for s in source], axis=0)
        queries = dot(wq[layer], mine, ((0,), (1,))).astype(BF16)
        for g in range(group):
            attend(layer, which[g], queries, g * block)
        current = latent if layer > 0 else x_ref
        x = jnp.concatenate([current[s] for s in source], axis=0).astype(F32)
        after_att = x + normalize(dot(context[...], wo[layer], ((0,), (0,))), gains_ref[layer, 1:2, :])
        middle = normalize(after_att, gains_ref[layer, 2:3, :]).astype(BF16)
        part = math.gcd(hidden_size, 512)
        down = None
        for f in range(0, hidden_size, part):
            hidden = gelu(dot(middle, wu[layer, :, f : f + part])).astype(BF16)
            term = dot(hidden, wd[layer, f : f + part, :])
            down = term if down is None else down + term
        result = (after_att + normalize(down, gains_ref[layer, 3:4, :]) + virtual[0:1, :]).astype(BF16)
        at = pl.ds(i * group, group)
        if last:
            out_ref[at] = result.reshape(group, block, width)
        else:
            latent[at] = result.reshape(group, block, width)
            wide = result.astype(F32)
            fresh = normalize(wide, gains_ref[layer + 1, 0:1, :]).astype(BF16)
            normed[layer + 1, at] = fresh.reshape(group, block, width)
            total_ref[0:1, :] = total_ref[0:1, :] + jnp.sum(wide, axis=0, keepdims=True)

    use(0, range(3))
    gather(0)
    use(0, range(3, count_w))
    total_ref[0:1, :] = jnp.zeros((1, width), F32)

    def sending_step(i, carry):
        block_step(0, i)

        def each(k, carry):
            stage(1, order(1, k))
            return carry

        def go(k, carry):
            far_out(1, order(1, k)).start()
            return carry

        lax.fori_loop(i * group, (i + 1) * group, each, 0)
        lax.fori_loop(i * group, (i + 1) * group, go, 0)
        return carry

    def rest(k, carry):
        stage(1, order(1, k))
        return carry

    def go_rest(k, carry):
        far_out(1, order(1, k)).start()
        return carry

    lax.fori_loop(0, steps, sending_step, 0)
    stage_edges(1)
    lax.fori_loop(blocks, peers - 1, rest, 0)
    send_edges(1)
    lax.fori_loop(blocks, peers - 1, go_rest, 0)
    stage_self(1)

    use(1, range(3))
    gather(1)
    use(1, range(3, count_w))

    def last_step(i, carry):
        block_step(1, i)
        return carry

    lax.fori_loop(0, steps, last_step, 0)

    for layer in range(layers):
        def drain(k, carry, layer=layer):
            to = order(layer, k)
            far_out(layer, to).wait_send()
            sum_out(layer, to).wait_send()
            return carry

        lax.fori_loop(0, peers - 1, drain, 0)
        halo_each(layer, lambda copy, side: copy.wait_send())


def body(node_features, nbr_table, nbr_count, send_block, w_query, w_key, w_value, w_out, w_up, w_down, w_virtual, gains):
    blocks, listed = nbr_table.shape
    own, width = node_features.shape
    block = own // blocks
    peers = lax.axis_size(AXIS)
    slots = send_block.shape[1]
    layers = w_query.shape[0]
    group = math.gcd(blocks, 4)
    near = 2 * HALO_B + blocks
    entries = near + peers * slots
    shapes = (peers, layers, blocks, block, width, slots, listed, group, own * peers)
    weights = (w_query, w_key, w_value, w_out, w_up, w_down, w_virtual)
    vmem, smem, hbm = (pl.BlockSpec(memory_space=s) for s in (pltpu.VMEM, pltpu.SMEM, pl.ANY))
    dma = pltpu.SemaphoreType.DMA
    scratch = [pltpu.VMEM(w.shape, BF16) for w in weights]
    scratch += [
        pltpu.VMEM((layers, blocks, block, width), BF16),
        pltpu.VMEM((blocks, block, width), BF16),
        pltpu.VMEM((entries, block, width), BF16),
        pltpu.VMEM((entries, width, block), BF16),
        pltpu.VMEM((width, group * block), BF16),
        pltpu.VMEM((layers, peers, slots * block, width), BF16),
        pltpu.VMEM((layers, peers, slots * block, width), BF16),
        pltpu.VMEM((layers, 2, HALO_B * block, width), BF16),
        pltpu.VMEM((layers, 2, HALO_B * block, width), BF16),
        pltpu.VMEM((layers, width // 128, 128), F32),
        pltpu.VMEM((layers, peers, width // 128, 128), F32),
        pltpu.VMEM((8, width), F32),
        pltpu.VMEM((16, width), F32),
        pltpu.SMEM((blocks,), jnp.int32),
        pltpu.SMEM((blocks,), jnp.int32),
        pltpu.SMEM((layers, entries), jnp.int32),
        dma((layers, len(weights))),
        dma((layers, peers)),
        dma((layers, peers)),
        dma((layers, 2)),
        dma((layers, 2)),
        dma((layers, peers)),
        dma((layers, peers)),
    ]
    return pl.pallas_call(
        functools.partial(kernel, shapes),
        out_shape=jax.ShapeDtypeStruct((blocks, block, width), BF16),
        in_specs=[smem, smem, smem, vmem, vmem] + [hbm] * len(weights),
        out_specs=vmem,
        scratch_shapes=scratch,
        compiler_params=pltpu.CompilerParams(collective_id=0, has_side_effects=True, vmem_limit_bytes=VMEM_LIMIT),
        name="processor",
    )(nbr_table, nbr_count, send_block.reshape(-1), node_features.reshape(blocks, block, width), gains, *weights).reshape(own, width)


def solution(mesh):
    across = P(("members", "row"), None)
    in_specs = (across, P("row", None), P("row"), P("row", None)) + (P(),) * 8
    return jax.shard_map(body, mesh=mesh, in_specs=in_specs, out_specs=across, check_vma=False)
```

time: 208 us -> 128 us (0.62)
  the two profiles are of different devices: /device:TPU:15 before, /device:TPU:0 now
where the time goes in v1:
time: 128 us
  Pallas kernels  126 us (98%)
  local copies, waits for them, and re-layouts  2.26 us (2%)
    pallas_call x1, Pallas kernels, body(): pl.pallas_call(functools.partial(kernel, shapes), out_shape=jax.ShapeDtyp...  126 us

profile of v1, /device:TPU:0, one launch (start us, length us, event | category | flops | bytes accessed | tf_op | source)
XLA Modules:
  0.0 128.2 jit_solution(5677046309830204644)
XLA Ops:
  0.0 125.9 %processor.1 = bf16[8,128,512]{2,1,0:T(8,128)(2,1)} custom-call(s32[8,8]{1,0:T(8,128)} %table_sm.1, s32[8]{0:T(128)} %count_sm.1, s32[16]{0:T(128)} %bitcast.5, bf16[8,128,512]{2,1,0:T(8,128)(2,1)} %bitcast.4, f32[2,4,512]{2,1,0:T(4,128)} %gains_ref.1, bf16[2,512,512]{2,1,0:T(8,128)(2,1)} %wq_hbm.1, bf16[2,512,512]{2,1,0:T(8,128)(2,1)} %wk_hbm.1, ...), custom_call_target="tpu_custom_call" | custom-call | tf_op jit(solution)/shard_map/processor/pallas_call | solution.py:446
  125.9 2.3 %copy.14 = bf16[1024,512]{1,0:T(8,128)(2,1)} copy(bf16[1024,512]{1,0:T(8,128)(2,1)} %bitcast.3) | data formatting | bytes 2097152

commit v2 on v1

--- a/solution.py
+++ b/solution.py
@@ -49,10 +49,50 @@
     return 1 - jnp.minimum(jnp.maximum(a - b, b - a), 1)
 
 
-def kernel(shapes, table_sm, count_sm, send_sm, x_ref, gains_ref, wq_hbm, wk_hbm, wv_hbm, wo_hbm, wu_hbm, wd_hbm,
-           wm_hbm, out_ref, wq, wk, wv, wo, wu, wd, wm, normed, latent, keys, values, context, send_buf, far,
-           halo_send, halo, sum_send, sums, total_ref, virtual, perm_sm, pos_sm, place_sm, w_sem, far_send, far_recv,
-           halo_ssem, halo_rsem, sum_ssem, sum_rsem):
+def attend(count, key_of, value_of, query_of, context, at, listed, head, block):
+    scale = math.log2(math.e) / math.sqrt(head)
+    dead = [(1 - below(j, count)).astype(F32) * -1e30 for j in range(listed)]
+    blank = jnp.zeros((head, block), BF16)
+    for h in range(0, HEADS, 2):
+        pair = slice(h * head, (h + 2) * head)
+        upper = query_of(slice(h * head, (h + 1) * head))
+        lower = query_of(slice((h + 1) * head, (h + 2) * head))
+        both = jnp.concatenate(
+            [jnp.concatenate([upper, blank], axis=1), jnp.concatenate([blank, lower], axis=1)], axis=0
+        )
+        scores = []
+        for j in range(listed):
+            s = dot(key_of(j, pair), both)
+            scores.append(s if 2 * j < listed else s + dead[j])
+        top = jnp.max(functools.reduce(jnp.maximum, scores), axis=0, keepdims=True)
+        weights = [jnp.exp2((s - top) * scale) for s in scores]
+        inverse = 1.0 / jnp.sum(functools.reduce(jnp.add, weights), axis=0, keepdims=True)
+        probs = jnp.concatenate([w.astype(BF16) for w in weights], axis=0)
+        mixed = dot(jnp.concatenate([value_of(j, pair) for j in range(listed)], axis=1), probs)
+        for n in range(2):
+            part = slice(n * block, (n + 1) * block)
+            of_head = slice((h + n) * head, (h + n + 1) * head)
+            context[of_head, at : at + block] = (mixed[n * head : (n + 1) * head, part] * inverse[:, part]).astype(BF16)
+
+
+def feed(x, context, wo, wu, wd, gains_ref, layer):
+    after_att = x + normalize(dot(context, wo, ((0,), (0,))), gains_ref[layer, 1:2, :])
+    middle = normalize(after_att, gains_ref[layer, 2:3, :]).astype(BF16)
+    hidden_size = wu.shape[-1]
+    part = math.gcd(hidden_size, 512)
+    down = None
+    for f in range(0, hidden_size, part):
+        hidden = gelu(dot(middle, wu[:, f : f + part])).astype(BF16)
+        term = dot(hidden, wd[f : f + part, :])
+        down = term if down is None else down + term
+    return after_att + normalize(down, gains_ref[layer, 3:4, :])
+
+
+def exchange_kernel(shapes, table_sm, count_sm, send_sm, gains_ref, x_hbm, wq_hbm, wk_hbm, wv_hbm, wo_hbm, wu_hbm,
+                    wd_hbm, wm_hbm, early_out, keys_out, values_out, queries_out, latent_out, virtual_ref, wq, wk, wv,
+                    wo, wu, wd, wm, x_ref, normed, latent, keys, values, context, send_buf, far, halo_send, halo,
+                    sum_send, sums, total_ref, early, asked, arranged, virtual, perm_sm, pos_sm, x_sem, w_sem, far_send,
+                    far_recv, halo_ssem, halo_rsem, sum_ssem, sum_rsem, table_sem, early_sem):
     peers, layers, blocks, block, width, slots, listed, group, node_total = shapes
     near = 2 * HALO_B + blocks
     bits = peers.bit_length() - 1
@@ -60,7 +100,6 @@
     rows = group * block
     steps = blocks // group
     head = width // HEADS
-    hidden_size = wu.shape[-1]
     me = lax.axis_index(AXIS)
     inner = jnp.where((me >= quarter) & (me < half + quarter), 1, 0)
 
@@ -69,9 +108,10 @@
         if layer == 0:
             inside = jnp.where(k < half - 1, half - 1 - k, peers - 1 - (k - (half - 1)))
         else:
-            late = k - quarter
+            lead = quarter // 2
+            late = k - lead
             inside = jnp.where(
-                late < 0, peers - 1 - k, jnp.where(late < half - 1, half - 1 - late, peers - 1 - quarter - (late - half + 1))
+                late < 0, peers - 1 - k, jnp.where(late < half - 1, half - 1 - late, peers - 1 - lead - (late - half + 1))
             )
         return flip(me, jnp.where(inner == 1, inside, outer), bits)
 
@@ -116,6 +156,8 @@
 
     lax.fori_loop(1, peers, greet, 0)
 
+    load_x = pltpu.make_async_copy(x_hbm, x_ref, x_sem)
+    load_x.start()
     loads = []
     for layer in range(layers):
         for n, (src, dst) in enumerate(
@@ -126,6 +168,7 @@
         load.start()
 
     total_ref[0:1, :] = jnp.zeros((1, width), F32)
+    load_x.wait()
 
     def first(i, carry):
         x = x_ref[pl.ds(i * group, group)].reshape(rows, width).astype(F32)
@@ -204,11 +247,6 @@
         for b in range(blocks):
             which = which + equal(places[b], n) * b
         perm_sm[n] = which
-    for t in range(near + peers * slots):
-        place_sm[0, t] = jnp.int32(t)
-        own_b = t - HALO_B
-        place_sm[1, t] = HALO_B + places[own_b] if 0 <= own_b < blocks else jnp.int32(t)
-
     count_w = 7
 
     def use(layer, names):
@@ -223,18 +261,40 @@
         for n in range(count):
             values[at + n] = turned[:, n * block : (n + 1) * block]
 
+    def export(at, count, n):
+        part = pl.ds(at, count)
+        return (
+            pltpu.make_async_copy(keys.at[part], keys_out.at[part], table_sem.at[0, n]),
+            pltpu.make_async_copy(values.at[part], values_out.at[part], table_sem.at[1, n]),
+        )
+
+    chunk = math.gcd(blocks, 4)
+    many = math.gcd(quarter, 4)
+    first_far = blocks // chunk + 2
+
+    def hand_on(layer, at, count, n):
+        if layer == layers - 1:
+            for copy in export(at, count, n):
+                copy.start()
+
     def gather(layer):
-        chunk = math.gcd(blocks, 4)
-
         def own_piece(i, carry):
-            project(layer, normed[layer, pl.ds(i * chunk, chunk)], HALO_B + i * chunk)
+            if layer == 0:
+                piece = normed[layer, pl.ds(i * chunk, chunk)]
+            else:
+                piece = jnp.concatenate([normed[layer, pos_sm[i * chunk + n]] for n in range(chunk)], axis=0)
+                piece = piece.reshape(chunk, block, width)
+            project(layer, piece, HALO_B + i * chunk)
+            hand_on(layer, HALO_B + i * chunk, chunk, i)
             return carry
 
         lax.fori_loop(0, blocks // chunk, own_piece, 0)
 
         def halo_in(copy, side):
             copy.wait_recv()
-            project(layer, halo[layer, side].reshape(HALO_B, block, width), 0 if side == 0 else HALO_B + blocks)
+            at = 0 if side == 0 else HALO_B + blocks
+            project(layer, halo[layer, side].reshape(HALO_B, block, width), at)
+            hand_on(layer, at, HALO_B, blocks // chunk + side)
 
         @pl.when(me > 0)
         def _():
@@ -244,7 +304,9 @@
         def _():
             halo_in(halo_copy(layer, 0, me + 1), 1)
 
-        many = math.gcd(quarter, 4)
+        if layer == layers - 1:
+            lax.fori_loop(0, steps, early_step, 0)
+            drain(0)
         for inside, outside in ((2, 0), (0, 1), (1, 3), (3, 2)):
             part = flip(lax.div(me, jnp.int32(quarter)), jnp.where(inner == 1, inside, outside), 2) * quarter
 
@@ -262,23 +324,22 @@
                 lax.fori_loop(i * many, (i + 1) * many, wait_one, 0)
                 piece = far[layer, pl.ds(source, many)].reshape(many * slots, block, width)
                 project(layer, piece, near + source * slots)
+                hand_on(layer, near + source * slots, many * slots, first_far + lax.div(source, jnp.int32(many)))
                 return carry
 
             lax.fori_loop(0, quarter // many, far_piece, 0)
 
         def sum_wait(k, carry):
-            sum_in(layer, order(layer, k)).wait_recv()
+            sum_in(layer, lax.rem(me + k, peers)).wait_recv()
             return carry
 
-        lax.fori_loop(0, peers - 1, sum_wait, 0)
+        lax.fori_loop(1, peers, sum_wait, 0)
         whole = jnp.sum(sums[layer], axis=0)
         mean = jnp.concatenate([whole[k : k + 1, :] for k in range(width // 128)], axis=1) / node_total
         mean = jnp.broadcast_to(mean, (16, width)).astype(BF16)
         virtual[...] = dot(mean, wm[layer])
 
-    scale = math.log2(math.e) / math.sqrt(head)
-
-    def attend(layer, which, queries, at):
+    def attend_in(layer, which, queries, at):
         count = count_sm[which]
         home = table_sm[which, 0]
         spots = []
@@ -286,32 +347,26 @@
             entry = table_sm[which, j]
             if 2 * j >= listed:
                 entry = home + below(j, count) * (entry - home)
-            spots.append(place_sm[layer, entry])
-        dead = [(1 - below(j, count)).astype(F32) * -1e30 for j in range(listed)]
-        blank = jnp.zeros((head, block), BF16)
-        for h in range(0, HEADS, 2):
-            pair = slice(h * head, (h + 2) * head)
-            upper = queries[h * head : (h + 1) * head, at : at + block]
-            lower = queries[(h + 1) * head : (h + 2) * head, at : at + block]
-            both = jnp.concatenate(
-                [jnp.concatenate([upper, blank], axis=1), jnp.concatenate([blank, lower], axis=1)], axis=0
-            )
-            scores = []
-            for j in range(listed):
-                s = dot(keys[spots[j], :, pair], both)
-                scores.append(s if 2 * j < listed else s + dead[j])
-            top = jnp.max(functools.reduce(jnp.maximum, scores), axis=0, keepdims=True)
-            weights = [jnp.exp2((s - top) * scale) for s in scores]
-            inverse = 1.0 / jnp.sum(functools.reduce(jnp.add, weights), axis=0, keepdims=True)
-            probs = jnp.concatenate([w.astype(BF16) for w in weights], axis=0)
-            v = jnp.concatenate([values[p, pair] for p in spots], axis=1)
-            mixed = dot(v, probs)
-            for n in range(2):
-                part = slice(n * block, (n + 1) * block)
-                of_head = slice((h + n) * head, (h + n + 1) * head)
-                context[of_head, at : at + block] = (
-                    mixed[n * head : (n + 1) * head, part] * inverse[:, part]
-                ).astype(BF16)
+            spots.append(entry)
+        attend(
+            count,
+            lambda j, pair: keys[spots[j], :, pair],
+            lambda j, pair: values[spots[j], pair],
+            lambda part: queries[part, at : at + block],
+            context,
+            at,
+            listed,
+            head,
+            block,
+        )
+
+    def early_copies(i):
+        at = pl.ds(i * group, group)
+        return (
+            pltpu.make_async_copy(early.at[at], early_out.at[at], early_sem.at[0, i]),
+            pltpu.make_async_copy(asked.at[at], queries_out.at[at], early_sem.at[1, i]),
+            pltpu.make_async_copy(arranged.at[at], latent_out.at[at], early_sem.at[2, i]),
+        )
 
     def block_step(layer, i):
         last = layer == layers - 1
@@ -319,34 +374,48 @@
         if last:
             which = order_at
             source = [pos_sm[w] for w in which]
+            for w, s in zip(which, source):
+                arranged[w] = latent[s]
         else:
             which = [perm_sm[n] for n in order_at]
             source = which
         mine = jnp.concatenate([normed[layer, s] for s in source], axis=0)
         queries = dot(wq[layer], mine, ((0,), (1,))).astype(BF16)
+        if last:
+            for g in range(group):
+                asked[which[g]] = queries[:, g * block : (g + 1) * block]
         for g in range(group):
-            attend(layer, which[g], queries, g * block)
+            attend_in(layer, which[g], queries, g * block)
         current = latent if layer > 0 else x_ref
         x = jnp.concatenate([current[s] for s in source], axis=0).astype(F32)
-        after_att = x + normalize(dot(context[...], wo[layer], ((0,), (0,))), gains_ref[layer, 1:2, :])
-        middle = normalize(after_att, gains_ref[layer, 2:3, :]).astype(BF16)
-        part = math.gcd(hidden_size, 512)
-        down = None
-        for f in range(0, hidden_size, part):
-            hidden = gelu(dot(middle, wu[layer, :, f : f + part])).astype(BF16)
-            term = dot(hidden, wd[layer, f : f + part, :])
-            down = term if down is None else down + term
-        result = (after_att + normalize(down, gains_ref[layer, 3:4, :]) + virtual[0:1, :]).astype(BF16)
+        result = feed(x, context[...], wo[layer], wu.at[layer], wd.at[layer], gains_ref, layer)
         at = pl.ds(i * group, group)
         if last:
-            out_ref[at] = result.reshape(group, block, width)
+            early[at] = result.reshape(group, block, width)
+            for copy in early_copies(i):
+                copy.start()
         else:
+            result = (result + virtual[0:1, :]).astype(BF16)
             latent[at] = result.reshape(group, block, width)
             wide = result.astype(F32)
             fresh = normalize(wide, gains_ref[layer + 1, 0:1, :]).astype(BF16)
             normed[layer + 1, at] = fresh.reshape(group, block, width)
             total_ref[0:1, :] = total_ref[0:1, :] + jnp.sum(wide, axis=0, keepdims=True)
 
+    def early_step(i, carry):
+        block_step(layers - 1, i)
+        return carry
+
+    def drain(layer):
+        def one(k, carry):
+            to = lax.rem(me + k, peers)
+            far_out(layer, to).wait_send()
+            sum_out(layer, to).wait_send()
+            return carry
+
+        lax.fori_loop(1, peers, one, 0)
+        halo_each(layer, lambda copy, side: copy.wait_send())
+
     use(0, range(3))
     gather(0)
     use(0, range(3, count_w))
@@ -355,6 +424,11 @@
     def sending_step(i, carry):
         block_step(0, i)
 
+        @pl.when(i == steps - 1)
+        def _():
+            stage_edges(1)
+            send_edges(1)
+
         def each(k, carry):
             stage(1, order(1, k))
             return carry
@@ -376,31 +450,139 @@
         return carry
 
     lax.fori_loop(0, steps, sending_step, 0)
-    stage_edges(1)
     lax.fori_loop(blocks, peers - 1, rest, 0)
-    send_edges(1)
     lax.fori_loop(blocks, peers - 1, go_rest, 0)
     stage_self(1)
 
-    use(1, range(3))
+    use(1, range(count_w))
     gather(1)
-    use(1, range(3, count_w))
-
-    def last_step(i, carry):
-        block_step(1, i)
-        return carry
-
-    lax.fori_loop(0, steps, last_step, 0)
-
-    for layer in range(layers):
-        def drain(k, carry, layer=layer):
-            to = order(layer, k)
-            far_out(layer, to).wait_send()
-            sum_out(layer, to).wait_send()
-            return carry
-
-        lax.fori_loop(0, peers - 1, drain, 0)
-        halo_each(layer, lambda copy, side: copy.wait_send())
+    virtual_ref[...] = virtual[...]
+
+    drain(1)
+
+    def await_own(n, carry):
+        for copy in export(HALO_B + n * chunk, chunk, n):
+            copy.wait()
+        return carry
+
+    def await_far(n, carry):
+        for copy in export(near + n * many * slots, many * slots, first_far + n):
+            copy.wait()
+        return carry
+
+    def await_early(n, carry):
+        for copy in early_copies(n):
+            copy.wait()
+        return carry
+
+    @pl.when(me > 0)
+    def _():
+        for copy in export(0, HALO_B, blocks // chunk):
+            copy.wait()
+
+    @pl.when(me < peers - 1)
+    def _():
+        for copy in export(HALO_B + blocks, HALO_B, blocks // chunk + 1):
+            copy.wait()
+
+    lax.fori_loop(0, blocks // chunk, await_own, 0)
+    lax.fori_loop(0, peers // many, await_far, 0)
+    lax.fori_loop(0, steps, await_early, 0)
+
+
+def finish_kernel(layer, near, group, table_sm, count_sm, gains_ref, virtual_ref, early_hbm, keys_hbm, values_hbm,
+                  queries_hbm, latent_hbm, wo_hbm, wu_hbm, wd_hbm, out_ref, early, kept_keys, kept_values, asked, current,
+                  context, wo, wu, wd, todo_sm, early_sem, w_sem, key_sem, value_sem, row_sem):
+    blocks, block, width = out_ref.shape
+    listed = table_sm.shape[1]
+    head = width // HEADS
+
+    load_early = pltpu.make_async_copy(early_hbm, early, early_sem)
+    weight_loads = [
+        pltpu.make_async_copy(src.at[layer], dst, w_sem.at[n])
+        for n, (src, dst) in enumerate(((wo_hbm, wo), (wu_hbm, wu), (wd_hbm, wd)))
+    ]
+
+    number = jnp.int32(0)
+    for b in range(blocks):
+        away = jnp.int32(0)
+        for j in range(listed):
+            away = jnp.where((j < count_sm[b]) & (table_sm[b, j] >= near), 1, away)
+
+        @pl.when(away > 0)
+        def _(b=b, number=number):
+            todo_sm[number] = b
+
+        number = number + away
+
+    def block_of(i, g):
+        return todo_sm[jnp.minimum(i * group + g, number - 1)]
+
+    def entry_of(which, j):
+        return jnp.where(j < count_sm[which], table_sm[which, j], table_sm[which, 0])
+
+    def copies(i, g):
+        which = block_of(i, g)
+        row = [
+            pltpu.make_async_copy(queries_hbm.at[which], asked.at[g], row_sem.at[0, g]),
+            pltpu.make_async_copy(latent_hbm.at[which], current.at[g], row_sem.at[1, g]),
+        ]
+        for j in range(listed):
+            entry = entry_of(which, j)
+            row.append(pltpu.make_async_copy(keys_hbm.at[entry], kept_keys.at[g, j], key_sem.at[g, j]))
+            row.append(pltpu.make_async_copy(values_hbm.at[entry], kept_values.at[g, j], value_sem.at[g, j]))
+        return row
+
+    @pl.when(number > 0)
+    def _():
+        for g in range(group):
+            for copy in copies(0, g):
+                copy.start()
+
+    load_early.start()
+    for load in weight_loads:
+        load.start()
+    load_early.wait()
+    shared = virtual_ref[0:1, :]
+
+    def settle(b, carry):
+        out_ref[b] = (early[b] + shared).astype(BF16)
+        return carry
+
+    lax.fori_loop(0, blocks, settle, 0)
+    for load in weight_loads:
+        load.wait()
+
+    def late_step(i, carry):
+        @pl.when(i > 0)
+        def _():
+            for g in range(group):
+                for copy in copies(i, g):
+                    copy.start()
+
+        for g in range(group):
+            which = block_of(i, g)
+            for copy in copies(i, g):
+                copy.wait()
+            attend(
+                count_sm[which],
+                lambda j, pair, g=g: kept_keys[g, j, :, pair],
+                lambda j, pair, g=g: kept_values[g, j, pair, :],
+                lambda part, g=g: asked[g, part, :],
+                context,
+                g * block,
+                listed,
+                head,
+                block,
+            )
+        x = current[...].reshape(group * block, width).astype(F32)
+        result = feed(x, context[...], wo[...], wu, wd, gains_ref, layer) + shared
+        result = result.astype(BF16).reshape(group, block, width)
+        for g in range(group):
+            out_ref[block_of(i, g)] = result[g]
+        return carry
+
+    lax.fori_loop(0, (number + group - 1) // group, late_step, 0)
 
 
 def body(node_features, nbr_table, nbr_count, send_block, w_query, w_key, w_value, w_out, w_up, w_down, w_virtual, gains):
@@ -417,8 +599,12 @@
     weights = (w_query, w_key, w_value, w_out, w_up, w_down, w_virtual)
     vmem, smem, hbm = (pl.BlockSpec(memory_space=s) for s in (pltpu.VMEM, pltpu.SMEM, pl.ANY))
     dma = pltpu.SemaphoreType.DMA
+    shape = jax.ShapeDtypeStruct
+    steps = blocks // group
+    groups = blocks // math.gcd(blocks, 4) + 2 + peers // math.gcd(peers // 4, 4)
     scratch = [pltpu.VMEM(w.shape, BF16) for w in weights]
     scratch += [
+        pltpu.VMEM((blocks, block, width), BF16),
         pltpu.VMEM((layers, blocks, block, width), BF16),
         pltpu.VMEM((blocks, block, width), BF16),
         pltpu.VMEM((entries, block, width), BF16),
@@ -431,10 +617,13 @@
         pltpu.VMEM((layers, width // 128, 128), F32),
         pltpu.VMEM((layers, peers, width // 128, 128), F32),
         pltpu.VMEM((8, width), F32),
+        pltpu.VMEM((blocks, block, width), F32),
+        pltpu.VMEM((blocks, width, block), BF16),
+        pltpu.VMEM((blocks, block, width), BF16),
         pltpu.VMEM((16, width), F32),
         pltpu.SMEM((blocks,), jnp.int32),
         pltpu.SMEM((blocks,), jnp.int32),
-        pltpu.SMEM((layers, entries), jnp.int32),
+        dma,
         dma((layers, len(weights))),
         dma((layers, peers)),
         dma((layers, peers)),
@@ -442,16 +631,51 @@
         dma((layers, 2)),
         dma((layers, peers)),
         dma((layers, peers)),
+        dma((2, groups)),
+        dma((3, steps)),
     ]
-    return pl.pallas_call(
-        functools.partial(kernel, shapes),
-        out_shape=jax.ShapeDtypeStruct((blocks, block, width), BF16),
-        in_specs=[smem, smem, smem, vmem, vmem] + [hbm] * len(weights),
-        out_specs=vmem,
+    early, keys, values, queries, latent, virtual = pl.pallas_call(
+        functools.partial(exchange_kernel, shapes),
+        out_shape=(
+            shape((blocks, block, width), F32),
+            shape((entries, block, width), BF16),
+            shape((entries, width, block), BF16),
+            shape((blocks, width, block), BF16),
+            shape((blocks, block, width), BF16),
+            shape((16, width), F32),
+        ),
+        in_specs=[smem, smem, smem, vmem] + [hbm] * (1 + len(weights)),
+        out_specs=(hbm, hbm, hbm, hbm, hbm, vmem),
         scratch_shapes=scratch,
         compiler_params=pltpu.CompilerParams(collective_id=0, has_side_effects=True, vmem_limit_bytes=VMEM_LIMIT),
-        name="processor",
-    )(nbr_table, nbr_count, send_block.reshape(-1), node_features.reshape(blocks, block, width), gains, *weights).reshape(own, width)
+        name="exchange",
+    )(nbr_table, nbr_count, send_block.reshape(-1), gains, node_features.reshape(blocks, block, width), *weights)
+    result = pl.pallas_call(
+        functools.partial(finish_kernel, layers - 1, near, group),
+        out_shape=shape((blocks, block, width), BF16),
+        in_specs=[smem, smem, vmem, vmem] + [hbm] * 8,
+        out_specs=vmem,
+        scratch_shapes=[
+            pltpu.VMEM((blocks, block, width), F32),
+            pltpu.VMEM((group, listed, block, width), BF16),
+            pltpu.VMEM((group, listed, width, block), BF16),
+            pltpu.VMEM((group, width, block), BF16),
+            pltpu.VMEM((group, block, width), BF16),
+            pltpu.VMEM((width, group * block), BF16),
+            pltpu.VMEM(w_out.shape[1:], BF16),
+            pltpu.VMEM(w_up.shape[1:], BF16),
+            pltpu.VMEM(w_down.shape[1:], BF16),
+            pltpu.SMEM((blocks,), jnp.int32),
+            dma,
+            dma((3,)),
+            dma((group, listed)),
+            dma((group, listed)),
+            dma((2, group)),
+        ],
+        compiler_params=pltpu.CompilerParams(vmem_limit_bytes=VMEM_LIMIT),
+        name="finish",
+    )(nbr_table, nbr_count, gains, virtual, early, keys, values, queries, latent, w_out, w_up, w_down)
+    return result.reshape(own, width)
 
 
 def solution(mesh):

time: 128 us -> 135 us (1.055)
  Pallas kernels: 126 us -> 134 us
  local copies, waits for them, and re-layouts: 2.26 us -> 0 us
    pallas_call x1 -> x2, Pallas kernels: 126 us -> 134 us  [the longest x1 116 us: body(): pl.pallas_call(functools.partial(exchange_kernel, shapes), out_shape=(sha...]
    unnamed x1 -> x0, local copies, waits for them, and re-layouts: 2.26 us -> none
where the time goes in v2:
time: 135 us; the launch traced here: 134 us
  Pallas kernels  134 us (99%)
    pallas_call x1, Pallas kernels, body(): pl.pallas_call(functools.partial(exchange_kernel, shapes), out_shape=(sha...  116 us
    pallas_call x1, Pallas kernels, body(): pl.pallas_call(functools.partial(finish_kernel, layers - 1, near, group),...  17.6 us

profile of v2, /device:TPU:0, one launch (start us, length us, event | category | flops | bytes accessed | tf_op | source)
XLA Modules:
  0.0 134.0 jit_solution(1621156097111315295)
XLA Ops:
  0.0 116.3 %exchange.1 = (f32[8,128,512]{2,1,0:T(8,128)}, bf16[28,128,512]{2,1,0:T(8,128)(2,1)}, bf16[28,512,128]{2,1,0:T(8,128)(2,1)}, bf16[8,512,128]{2,1,0:T(8,128)(2,1)...) custom-call(s32[8,8]{1,0:T(8,128)} %table_sm.3, s32[8]{0:T(128)} %count_sm.3, s32[16]{0:T(128)} %bitcast.4, ...), custom_call_target="tpu_custom_call" | custom-call | tf_op jit(solution)/shard_map/exchange/pallas_call | solution.py:637
  116.3 17.6 %finish.1 = bf16[8,128,512]{2,1,0:T(8,128)(2,1)} custom-call(s32[8,8]{1,0:T(8,128)} %table_sm.3, s32[8]{0:T(128)} %count_sm.3, f32[2,4,512]{2,1,0:T(4,128)} %gains_ref.3, f32[16,512]{1,0:T(8,128)} %get-tuple-element.11.virtual_ref, f32[8,128,512]{2,1,0:T(8,128)} %get-tuple-element.12.early_hbm, bf16[28,128,512]{2,1,0:T(8,128)(2,1)} %get-tuple-element.13.keys_hbm, ...), custom_call_target="tpu_custom_call" | custom-call | tf_op jit(solution)/shard_map/finish/pallas_call | solution.py:653

commit v3 on v2

--- a/solution.py
+++ b/solution.py
@@ -89,7 +89,7 @@
 
 
 def exchange_kernel(shapes, table_sm, count_sm, send_sm, gains_ref, x_hbm, wq_hbm, wk_hbm, wv_hbm, wo_hbm, wu_hbm,
-                    wd_hbm, wm_hbm, early_out, keys_out, values_out, queries_out, latent_out, virtual_ref, wq, wk, wv,
+                    wd_hbm, wm_hbm, settled_out, keys_out, values_out, queries_out, latent_out, virtual_ref, wq, wk, wv,
                     wo, wu, wd, wm, x_ref, normed, latent, keys, values, context, send_buf, far, halo_send, halo,
                     sum_send, sums, total_ref, early, asked, arranged, virtual, perm_sm, pos_sm, x_sem, w_sem, far_send,
                     far_recv, halo_ssem, halo_rsem, sum_ssem, sum_rsem, table_sem, early_sem):
@@ -108,7 +108,7 @@
         if layer == 0:
             inside = jnp.where(k < half - 1, half - 1 - k, peers - 1 - (k - (half - 1)))
         else:
-            lead = quarter // 2
+            lead = quarter
             late = k - lead
             inside = jnp.where(
                 late < 0, peers - 1 - k, jnp.where(late < half - 1, half - 1 - late, peers - 1 - lead - (late - half + 1))
@@ -139,15 +139,21 @@
             halo_send.at[layer, side], halo.at[layer, 1 - side], halo_ssem.at[layer, side], halo_rsem.at[layer, 1 - side], to
         )
 
-    def halo_each(layer, act):
-        @pl.when(me > 0)
-        def _():
-            act(halo_copy(layer, 0, me - 1), 0)
-
-        @pl.when(me < peers - 1)
-        def _():
-            act(halo_copy(layer, 1, me + 1), 1)
-
+    middle_side = [jnp.where(me == half, 1, 0), jnp.where(me == half - 1, 1, 0)]
+    middle = middle_side[0] + middle_side[1]
+
+    def halo_each(act, across=None):
+        for side in range(2):
+            there = me > 0 if side == 0 else me < peers - 1
+            if across is not None:
+                there = there & (middle_side[side] == across)
+
+            @pl.when(there)
+            def _(side=side):
+                act(side, me - 1 if side == 0 else me + 1)
+
+    load_x = pltpu.make_async_copy(x_hbm, x_ref, x_sem)
+    load_x.start()
     barrier = pltpu.get_barrier_semaphore()
 
     def greet(k, carry):
@@ -155,20 +161,16 @@
         return carry
 
     lax.fori_loop(1, peers, greet, 0)
-
-    load_x = pltpu.make_async_copy(x_hbm, x_ref, x_sem)
-    load_x.start()
     loads = []
     for layer in range(layers):
         for n, (src, dst) in enumerate(
             ((wk_hbm, wk), (wv_hbm, wv), (wm_hbm, wm), (wq_hbm, wq), (wo_hbm, wo), (wu_hbm, wu), (wd_hbm, wd))
         ):
             loads.append(pltpu.make_async_copy(src.at[layer], dst.at[layer], w_sem.at[layer, n]))
+    total_ref[0:1, :] = jnp.zeros((1, width), F32)
+    load_x.wait()
     for load in loads:
         load.start()
-
-    total_ref[0:1, :] = jnp.zeros((1, width), F32)
-    load_x.wait()
 
     def first(i, carry):
         x = x_ref[pl.ds(i * group, group)].reshape(rows, width).astype(F32)
@@ -193,25 +195,29 @@
                 at = pos_sm[at]
             far[layer, me, pl.ds(slot * block, block), :] = normed[layer, at]
 
-    def stage_edges(layer):
-        for side in range(2):
-            for b in range(HALO_B):
-                at = b if side == 0 else blocks - HALO_B + b
-                if layer > 0:
-                    at = pos_sm[at]
-                halo_send[layer, side, pl.ds(b * block, block), :] = normed[layer, at]
+    def stage_halo(layer, side):
+        for b in range(HALO_B):
+            at = b if side == 0 else blocks - HALO_B + b
+            if layer > 0:
+                at = pos_sm[at]
+            halo_send[layer, side, pl.ds(b * block, block), :] = normed[layer, at]
+
+    def send_halo(layer, across=None):
+        halo_each(lambda side, to: stage_halo(layer, side), across)
+        halo_each(lambda side, to: halo_copy(layer, side, to).start(), across)
+
+    def stage_sum(layer):
         for k in range(width // 128):
             part = total_ref[0:1, k * 128 : (k + 1) * 128]
             sum_send[layer, k : k + 1, :] = part
             sums[layer, me, k : k + 1, :] = part
 
-    def send_edges(layer):
+    def send_sum(layer):
         def one(k, carry):
-            sum_out(layer, order(layer, k)).start()
+            sum_out(layer, lax.rem(me + k, peers)).start()
             return carry
 
-        lax.fori_loop(0, peers - 1, one, 0)
-        halo_each(layer, lambda copy, side: copy.start())
+        lax.fori_loop(1, peers, one, 0)
 
     def stage_all(k, carry):
         stage(0, order(0, k))
@@ -221,10 +227,11 @@
         far_out(0, order(0, k)).start()
         return carry
 
-    stage_edges(0)
+    stage_sum(0)
     lax.fori_loop(0, peers - 1, stage_all, 0)
     pl.semaphore_wait(barrier, peers - 1)
-    send_edges(0)
+    send_halo(0)
+    send_sum(0)
     lax.fori_loop(0, peers - 1, send_all, 0)
     stage_self(0)
 
@@ -234,6 +241,10 @@
         for slot in range(slots - 1, -1, -1):
             b = send_sm[to * slots + slot]
             uses = [use + equal(b, n) * (k * slots + slot - use) for n, use in enumerate(uses)]
+    for n in range(HALO_B):
+        low, high = n, blocks - HALO_B + n
+        uses[low] = uses[low] - middle_side[0] * 2 * peers * slots
+        uses[high] = uses[high] - middle_side[1] * 2 * peers * slots
     places = []
     for n in range(blocks):
         place = jnp.int32(0)
@@ -363,9 +374,8 @@
     def early_copies(i):
         at = pl.ds(i * group, group)
         return (
-            pltpu.make_async_copy(early.at[at], early_out.at[at], early_sem.at[0, i]),
-            pltpu.make_async_copy(asked.at[at], queries_out.at[at], early_sem.at[1, i]),
-            pltpu.make_async_copy(arranged.at[at], latent_out.at[at], early_sem.at[2, i]),
+            pltpu.make_async_copy(asked.at[at], queries_out.at[at], early_sem.at[0, i]),
+            pltpu.make_async_copy(arranged.at[at], latent_out.at[at], early_sem.at[1, i]),
         )
 
     def block_step(layer, i):
@@ -414,7 +424,7 @@
             return carry
 
         lax.fori_loop(1, peers, one, 0)
-        halo_each(layer, lambda copy, side: copy.wait_send())
+        halo_each(lambda side, to: halo_copy(layer, side, to).wait_send())
 
     use(0, range(3))
     gather(0)
@@ -424,11 +434,19 @@
     def sending_step(i, carry):
         block_step(0, i)
 
+        @pl.when(i == 0)
+        def _():
+            send_halo(1, 1)
+
         @pl.when(i == steps - 1)
         def _():
-            stage_edges(1)
-            send_edges(1)
-
+            stage_sum(1)
+            send_halo(1, 0)
+            send_sum(1)
+
+        held = HALO_B * middle
+        begin = jnp.maximum(i * group - held, 0)
+        end = (i + 1) * group - held
         def each(k, carry):
             stage(1, order(1, k))
             return carry
@@ -437,8 +455,8 @@
             far_out(1, order(1, k)).start()
             return carry
 
-        lax.fori_loop(i * group, (i + 1) * group, each, 0)
-        lax.fori_loop(i * group, (i + 1) * group, go, 0)
+        lax.fori_loop(begin, end, each, 0)
+        lax.fori_loop(begin, end, go, 0)
         return carry
 
     def rest(k, carry):
@@ -450,14 +468,21 @@
         return carry
 
     lax.fori_loop(0, steps, sending_step, 0)
-    lax.fori_loop(blocks, peers - 1, rest, 0)
-    lax.fori_loop(blocks, peers - 1, go_rest, 0)
+    lax.fori_loop(blocks - HALO_B * middle, peers - 1, rest, 0)
+    lax.fori_loop(blocks - HALO_B * middle, peers - 1, go_rest, 0)
     stage_self(1)
 
     use(1, range(count_w))
     gather(1)
     virtual_ref[...] = virtual[...]
-
+    settled = pltpu.make_async_copy(latent, settled_out, x_sem)
+
+    def settle(b, carry):
+        latent[b] = (early[b] + virtual[0:1, :]).astype(BF16)
+        return carry
+
+    lax.fori_loop(0, blocks, settle, 0)
+    settled.start()
     drain(1)
 
     def await_own(n, carry):
@@ -488,21 +513,21 @@
     lax.fori_loop(0, blocks // chunk, await_own, 0)
     lax.fori_loop(0, peers // many, await_far, 0)
     lax.fori_loop(0, steps, await_early, 0)
-
-
-def finish_kernel(layer, near, group, table_sm, count_sm, gains_ref, virtual_ref, early_hbm, keys_hbm, values_hbm,
-                  queries_hbm, latent_hbm, wo_hbm, wu_hbm, wd_hbm, out_ref, early, kept_keys, kept_values, asked, current,
-                  context, wo, wu, wd, todo_sm, early_sem, w_sem, key_sem, value_sem, row_sem):
-    blocks, block, width = out_ref.shape
+    settled.wait()
+
+
+def finish_kernel(layer, near, group, table_sm, count_sm, gains_ref, virtual_ref, settled_hbm, keys_hbm, values_hbm,
+                  queries_hbm, latent_hbm, wo_hbm, wu_hbm, wd_hbm, out_hbm, kept_keys, kept_values, asked, current, fresh,
+                  context, kept, wo, wu, wd, todo_sm, away_sm, w_sem, key_sem, value_sem, row_sem, out_sem,
+                  kept_sem, keep_sem):
+    blocks = table_sm.shape[0]
+    block, width = current.shape[1:]
     listed = table_sm.shape[1]
     head = width // HEADS
-
-    load_early = pltpu.make_async_copy(early_hbm, early, early_sem)
     weight_loads = [
         pltpu.make_async_copy(src.at[layer], dst, w_sem.at[n])
         for n, (src, dst) in enumerate(((wo_hbm, wo), (wu_hbm, wu), (wd_hbm, wd)))
     ]
-
     number = jnp.int32(0)
     for b in range(blocks):
         away = jnp.int32(0)
@@ -513,61 +538,49 @@
         def _(b=b, number=number):
             todo_sm[number] = b
 
+        away_sm[b] = away
         number = number + away
+
+    load_kept = pltpu.make_async_copy(settled_hbm, kept, kept_sem)
+
+    def keep(b, act):
+        @pl.when(away_sm[b] == 0)
+        def _():
+            act(pltpu.make_async_copy(kept.at[b], out_hbm.at[b], keep_sem.at[b]))
 
     def block_of(i, g):
         return todo_sm[jnp.minimum(i * group + g, number - 1)]
 
-    def entry_of(which, j):
-        return jnp.where(j < count_sm[which], table_sm[which, j], table_sm[which, 0])
-
-    def copies(i, g):
+    def fetch(i, g, act):
         which = block_of(i, g)
-        row = [
-            pltpu.make_async_copy(queries_hbm.at[which], asked.at[g], row_sem.at[0, g]),
-            pltpu.make_async_copy(latent_hbm.at[which], current.at[g], row_sem.at[1, g]),
-        ]
+        act(pltpu.make_async_copy(queries_hbm.at[which], asked.at[g], row_sem.at[0, g]))
+        act(pltpu.make_async_copy(latent_hbm.at[which], current.at[g], row_sem.at[1, g]))
         for j in range(listed):
-            entry = entry_of(which, j)
-            row.append(pltpu.make_async_copy(keys_hbm.at[entry], kept_keys.at[g, j], key_sem.at[g, j]))
-            row.append(pltpu.make_async_copy(values_hbm.at[entry], kept_values.at[g, j], value_sem.at[g, j]))
-        return row
-
-    @pl.when(number > 0)
-    def _():
+            def one(j=j):
+                entry = table_sm[which, j]
+                act(pltpu.make_async_copy(keys_hbm.at[entry], kept_keys.at[g, j], key_sem.at[g, j]))
+                act(pltpu.make_async_copy(values_hbm.at[entry], kept_values.at[g, j], value_sem.at[g, j]))
+
+            if 2 * j < listed:
+                one()
+            else:
+                pl.when(j < count_sm[which])(one)
+
+    def begin(i):
         for g in range(group):
-            for copy in copies(0, g):
-                copy.start()
-
-    load_early.start()
-    for load in weight_loads:
-        load.start()
-    load_early.wait()
-    shared = virtual_ref[0:1, :]
-
-    def settle(b, carry):
-        out_ref[b] = (early[b] + shared).astype(BF16)
-        return carry
-
-    lax.fori_loop(0, blocks, settle, 0)
-    for load in weight_loads:
-        load.wait()
+            fetch(i, g, lambda copy: copy.start())
 
     def late_step(i, carry):
-        @pl.when(i > 0)
-        def _():
-            for g in range(group):
-                for copy in copies(i, g):
-                    copy.start()
-
+        pl.when(i > 0)(lambda: begin(i))
         for g in range(group):
             which = block_of(i, g)
-            for copy in copies(i, g):
-                copy.wait()
+            count = count_sm[which]
+            fetch(i, g, lambda copy: copy.wait())
+            spots = [j * below(j, count) for j in range(listed)]
             attend(
-                count_sm[which],
-                lambda j, pair, g=g: kept_keys[g, j, :, pair],
-                lambda j, pair, g=g: kept_values[g, j, pair, :],
+                count,
+                lambda j, pair, g=g, spots=spots: kept_keys[g, spots[j], :, pair],
+                lambda j, pair, g=g, spots=spots: kept_values[g, spots[j], pair, :],
                 lambda part, g=g: asked[g, part, :],
                 context,
                 g * block,
@@ -575,14 +588,45 @@
                 head,
                 block,
             )
+
+        @pl.when(i == 0)
+        def _():
+            load_kept.wait()
+            for b in range(blocks):
+                keep(b, lambda copy: copy.start())
+            for load in weight_loads:
+                load.wait()
+
         x = current[...].reshape(group * block, width).astype(F32)
-        result = feed(x, context[...], wo[...], wu, wd, gains_ref, layer) + shared
-        result = result.astype(BF16).reshape(group, block, width)
+        result = feed(x, context[...], wo[...], wu, wd, gains_ref, layer) + virtual_ref[0:1, :]
+        fresh[...] = result.astype(BF16).reshape(group, block, width)
+
+        def put(g):
+            return pltpu.make_async_copy(fresh.at[g], out_hbm.at[block_of(i, g)], out_sem.at[g])
+
         for g in range(group):
-            out_ref[block_of(i, g)] = result[g]
-        return carry
-
-    lax.fori_loop(0, (number + group - 1) // group, late_step, 0)
+            pl.when(i * group + g < number)(lambda g=g: put(g).start())
+        for g in range(group):
+            pl.when(i * group + g < number)(lambda g=g: put(g).wait())
+        return carry
+
+    @pl.when(number > 0)
+    def _():
+        begin(0)
+        load_kept.start()
+        for load in weight_loads:
+            load.start()
+        lax.fori_loop(0, (number + group - 1) // group, late_step, 0)
+
+    @pl.when(number == 0)
+    def _():
+        load_kept.start()
+        load_kept.wait()
+        for b in range(blocks):
+            keep(b, lambda copy: copy.start())
+
+    for b in range(blocks):
+        keep(b, lambda copy: copy.wait())
 
 
 def body(node_features, nbr_table, nbr_count, send_block, w_query, w_key, w_value, w_out, w_up, w_down, w_virtual, gains):
@@ -632,12 +676,12 @@
         dma((layers, peers)),
         dma((layers, peers)),
         dma((2, groups)),
-        dma((3, steps)),
+        dma((2, steps)),
     ]
-    early, keys, values, queries, latent, virtual = pl.pallas_call(
+    settled, keys, values, queries, latent, virtual = pl.pallas_call(
         functools.partial(exchange_kernel, shapes),
         out_shape=(
-            shape((blocks, block, width), F32),
+            shape((blocks, block, width), BF16),
             shape((entries, block, width), BF16),
             shape((entries, width, block), BF16),
             shape((blocks, width, block), BF16),
@@ -654,27 +698,31 @@
         functools.partial(finish_kernel, layers - 1, near, group),
         out_shape=shape((blocks, block, width), BF16),
         in_specs=[smem, smem, vmem, vmem] + [hbm] * 8,
-        out_specs=vmem,
+        out_specs=hbm,
         scratch_shapes=[
-            pltpu.VMEM((blocks, block, width), F32),
             pltpu.VMEM((group, listed, block, width), BF16),
             pltpu.VMEM((group, listed, width, block), BF16),
             pltpu.VMEM((group, width, block), BF16),
             pltpu.VMEM((group, block, width), BF16),
+            pltpu.VMEM((group, block, width), BF16),
             pltpu.VMEM((width, group * block), BF16),
+            pltpu.VMEM((blocks, block, width), BF16),
             pltpu.VMEM(w_out.shape[1:], BF16),
             pltpu.VMEM(w_up.shape[1:], BF16),
             pltpu.VMEM(w_down.shape[1:], BF16),
             pltpu.SMEM((blocks,), jnp.int32),
-            dma,
+            pltpu.SMEM((blocks,), jnp.int32),
             dma((3,)),
             dma((group, listed)),
             dma((group, listed)),
             dma((2, group)),
+            dma((group,)),
+            dma,
+            dma((blocks,)),
         ],
         compiler_params=pltpu.CompilerParams(vmem_limit_bytes=VMEM_LIMIT),
         name="finish",
-    )(nbr_table, nbr_count, gains, virtual, early, keys, values, queries, latent, w_out, w_up, w_down)
+    )(nbr_table, nbr_count, gains, virtual, settled, keys, values, queries, latent, w_out, w_up, w_down)
     return result.reshape(own, width)
 
 

time: 135 us -> 126 us (0.933)
  Pallas kernels: 134 us -> 125 us
    pallas_call x1, Pallas kernels: 116 us -> 110 us  [body(): pl.pallas_call(functools.partial(exchange_kernel, shapes), out_shape=(sha...]
    pallas_call x1, Pallas kernels: 17.6 us -> 14.2 us  [body(): pl.pallas_call(functools.partial(finish_kernel, layers - 1, near, group),...]
where the time goes in v3:
time: 126 us; the launch traced here: 125 us
  Pallas kernels  125 us (99%)
    pallas_call x1, Pallas kernels, body(): pl.pallas_call(functools.partial(exchange_kernel, shapes), out_shape=(sha...  110 us
    pallas_call x1, Pallas kernels, body(): pl.pallas_call(functools.partial(finish_kernel, layers - 1, near, group),...  14.2 us

profile of v3, /device:TPU:0, one launch (start us, length us, event | category | flops | bytes accessed | tf_op | source)
XLA Modules:
  0.0 124.7 jit_solution(6754758230149555136)
XLA Ops:
  0.0 110.3 %exchange.1 = (bf16[8,128,512]{2,1,0:T(8,128)(2,1)}, bf16[28,128,512]{2,1,0:T(8,128)(2,1)}, bf16[28,512,128]{2,1,0:T(8,128)(2,1)}, bf16[8,512,128]{2,1,0:T(8,128...) custom-call(s32[8,8]{1,0:T(8,128)} %table_sm.3, s32[8]{0:T(128)} %count_sm.3, s32[16]{0:T(128)} %bitcast.4, ...), custom_call_target="tpu_custom_call" | custom-call | tf_op jit(solution)/shard_map/exchange/pallas_call | solution.py:681
  110.3 14.2 %finish.1 = bf16[8,128,512]{2,1,0:T(8,128)(2,1)} custom-call(s32[8,8]{1,0:T(8,128)} %table_sm.3, s32[8]{0:T(128)} %count_sm.3, f32[2,4,512]{2,1,0:T(4,128)} %gains_ref.3, f32[16,512]{1,0:T(8,128)} %get-tuple-element.11.virtual_ref, bf16[8,128,512]{2,1,0:T(8,128)(2,1)} %get-tuple-element.12.settled_hbm, bf16[28,128,512]{2,1,0:T(8,128)(2,1)} %get-tuple-element.13.keys_hbm, ...), custom_call_target="tpu_custom_call" | custom-call | tf_op jit(solution)/shard_map/finish/pallas_call | solution.py:697

commit v4 on v3

--- a/solution.py
+++ b/solution.py
@@ -88,10 +88,11 @@
     return after_att + normalize(down, gains_ref[layer, 3:4, :])
 
 
-def exchange_kernel(shapes, table_sm, count_sm, send_sm, gains_ref, x_hbm, wq_hbm, wk_hbm, wv_hbm, wo_hbm, wu_hbm,
+def exchange_kernel(shapes, table_hbm, count_hbm, send_hbm, gains_hbm, x_hbm, wq_hbm, wk_hbm, wv_hbm, wo_hbm, wu_hbm,
                     wd_hbm, wm_hbm, settled_out, keys_out, values_out, queries_out, latent_out, virtual_ref, wq, wk, wv,
                     wo, wu, wd, wm, x_ref, normed, latent, keys, values, context, send_buf, far, halo_send, halo,
-                    sum_send, sums, total_ref, early, asked, arranged, virtual, perm_sm, pos_sm, x_sem, w_sem, far_send,
+                    sum_send, sums, total_ref, early, asked, arranged, virtual, table_sm, count_sm, send_sm,
+                    gains_ref, perm_sm, pos_sm, x_sem, small_sem, w_sem, far_send,
                     far_recv, halo_ssem, halo_rsem, sum_ssem, sum_rsem, table_sem, early_sem):
     peers, layers, blocks, block, width, slots, listed, group, node_total = shapes
     near = 2 * HALO_B + blocks
@@ -105,14 +106,11 @@
 
     def order(layer, k):
         outer = jnp.where(k < half, half + k, peers - 1 - k)
-        if layer == 0:
-            inside = jnp.where(k < half - 1, half - 1 - k, peers - 1 - (k - (half - 1)))
-        else:
-            lead = quarter
-            late = k - lead
-            inside = jnp.where(
-                late < 0, peers - 1 - k, jnp.where(late < half - 1, half - 1 - late, peers - 1 - lead - (late - half + 1))
-            )
+        lead = quarter // 2 if layer == 0 else quarter
+        late = k - lead
+        inside = jnp.where(
+            late < 0, peers - 1 - k, jnp.where(late < half - 1, half - 1 - late, peers - 1 - lead - (late - half + 1))
+        )
         return flip(me, jnp.where(inner == 1, inside, outer), bits)
 
     def remote(src, dst, ssem, rsem, to):
@@ -120,19 +118,21 @@
             src_ref=src, dst_ref=dst, send_sem=ssem, recv_sem=rsem, device_id={AXIS: to}, device_id_type=MESH
         )
 
+    my_part = lax.div(me, jnp.int32(quarter))
+
     def far_out(layer, to):
-        return remote(send_buf.at[layer, to], far.at[layer, me], far_send.at[layer, to], far_recv.at[layer, me], to)
-
-    def far_in(layer, source):
-        return remote(
-            send_buf.at[layer, source], far.at[layer, source], far_send.at[layer, source], far_recv.at[layer, source], source
-        )
+        return remote(send_buf.at[layer, to], far.at[layer, me], far_send.at[layer], far_recv.at[layer, my_part], to)
+
+    def far_some(layer, start, count, part):
+        some = pl.ds(start, count)
+        return remote(send_buf.at[layer, some], far.at[layer, some], far_send.at[layer], far_recv.at[layer, part], me)
 
     def sum_out(layer, to):
-        return remote(sum_send.at[layer], sums.at[layer, me], sum_ssem.at[layer, to], sum_rsem.at[layer, me], to)
-
-    def sum_in(layer, source):
-        return remote(sum_send.at[layer], sums.at[layer, source], sum_ssem.at[layer, source], sum_rsem.at[layer, source], source)
+        return remote(sum_send.at[layer], sums.at[layer, me], sum_ssem.at[layer], sum_rsem.at[layer], to)
+
+    def sum_all(layer):
+        some = sums.at[layer, pl.ds(0, peers - 1)]
+        return remote(some, some, sum_ssem.at[layer], sum_rsem.at[layer], me)
 
     def halo_copy(layer, side, to):
         return remote(
@@ -154,6 +154,14 @@
 
     load_x = pltpu.make_async_copy(x_hbm, x_ref, x_sem)
     load_x.start()
+    smalls = [
+        pltpu.make_async_copy(src, dst, small_sem.at[n])
+        for n, (src, dst) in enumerate(
+            ((gains_hbm, gains_ref), (send_hbm, send_sm), (table_hbm, table_sm), (count_hbm, count_sm))
+        )
+    ]
+    for small in smalls:
+        small.start()
     barrier = pltpu.get_barrier_semaphore()
 
     def greet(k, carry):
@@ -162,13 +170,14 @@
 
     lax.fori_loop(1, peers, greet, 0)
     loads = []
-    for layer in range(layers):
-        for n, (src, dst) in enumerate(
-            ((wk_hbm, wk), (wv_hbm, wv), (wm_hbm, wm), (wq_hbm, wq), (wo_hbm, wo), (wu_hbm, wu), (wd_hbm, wd))
-        ):
-            loads.append(pltpu.make_async_copy(src.at[layer], dst.at[layer], w_sem.at[layer, n]))
+    for n, (src, dst) in enumerate(
+        ((wk_hbm, wk), (wv_hbm, wv), (wm_hbm, wm), (wq_hbm, wq), (wo_hbm, wo), (wu_hbm, wu), (wd_hbm, wd))
+    ):
+        loads.append(pltpu.make_async_copy(src, dst, w_sem.at[n]))
     total_ref[0:1, :] = jnp.zeros((1, width), F32)
     load_x.wait()
+    for small in smalls:
+        small.wait()
     for load in loads:
         load.start()
 
@@ -258,12 +267,6 @@
         for b in range(blocks):
             which = which + equal(places[b], n) * b
         perm_sm[n] = which
-    count_w = 7
-
-    def use(layer, names):
-        for n in names:
-            loads[layer * count_w + n].wait()
-
     def project(layer, piece, at):
         count = piece.shape[0]
         flat = piece.reshape(count * block, width)
@@ -281,7 +284,6 @@
 
     chunk = math.gcd(blocks, 4)
     many = math.gcd(quarter, 4)
-    first_far = blocks // chunk + 2
 
     def hand_on(layer, at, count, n):
         if layer == layers - 1:
@@ -296,7 +298,7 @@
                 piece = jnp.concatenate([normed[layer, pos_sm[i * chunk + n]] for n in range(chunk)], axis=0)
                 piece = piece.reshape(chunk, block, width)
             project(layer, piece, HALO_B + i * chunk)
-            hand_on(layer, HALO_B + i * chunk, chunk, i)
+            hand_on(layer, HALO_B + i * chunk, chunk, 0)
             return carry
 
         lax.fori_loop(0, blocks // chunk, own_piece, 0)
@@ -305,7 +307,7 @@
             copy.wait_recv()
             at = 0 if side == 0 else HALO_B + blocks
             project(layer, halo[layer, side].reshape(HALO_B, block, width), at)
-            hand_on(layer, at, HALO_B, blocks // chunk + side)
+            hand_on(layer, at, HALO_B, 2 + side)
 
         @pl.when(me > 0)
         def _():
@@ -318,37 +320,36 @@
         if layer == layers - 1:
             lax.fori_loop(0, steps, early_step, 0)
             drain(0)
-        for inside, outside in ((2, 0), (0, 1), (1, 3), (3, 2)):
-            part = flip(lax.div(me, jnp.int32(quarter)), jnp.where(inner == 1, inside, outside), 2) * quarter
-
-            def wait_one(n, carry, part=part):
-                source = part + n
-
-                @pl.when(source != me)
-                def _():
-                    far_in(layer, source).wait_recv()
-
-                return carry
-
-            def far_piece(i, carry, part=part):
-                source = part + i * many
-                lax.fori_loop(i * many, (i + 1) * many, wait_one, 0)
+        for n, (inside, outside) in enumerate(((2, 0), (0, 1), (1, 3), (3, 2))):
+            if n == 3:
+                sum_all(layer).wait_recv()
+                whole = jnp.sum(sums[layer], axis=0)
+                mean = jnp.concatenate([whole[k : k + 1, :] for k in range(width // 128)], axis=1) / node_total
+                mean = jnp.broadcast_to(mean, (16, width)).astype(BF16)
+                virtual[...] = dot(mean, wm[layer])
+                if layer == layers - 1:
+                    virtual_ref[...] = virtual[...]
+                    lax.fori_loop(0, blocks, settle, 0)
+                    settled.start()
+            part = flip(my_part, jnp.where(inner == 1, inside, outside), 2)
+            start = part * quarter
+
+            @pl.when(part == my_part)
+            def _(part=part, start=start):
+                far_some(layer, start, quarter - 1, part).wait_recv()
+
+            @pl.when(part != my_part)
+            def _(part=part, start=start):
+                far_some(layer, start, quarter, part).wait_recv()
+
+            def far_piece(i, carry, start=start):
+                source = start + i * many
                 piece = far[layer, pl.ds(source, many)].reshape(many * slots, block, width)
                 project(layer, piece, near + source * slots)
-                hand_on(layer, near + source * slots, many * slots, first_far + lax.div(source, jnp.int32(many)))
+                hand_on(layer, near + source * slots, many * slots, 1)
                 return carry
 
             lax.fori_loop(0, quarter // many, far_piece, 0)
-
-        def sum_wait(k, carry):
-            sum_in(layer, lax.rem(me + k, peers)).wait_recv()
-            return carry
-
-        lax.fori_loop(1, peers, sum_wait, 0)
-        whole = jnp.sum(sums[layer], axis=0)
-        mean = jnp.concatenate([whole[k : k + 1, :] for k in range(width // 128)], axis=1) / node_total
-        mean = jnp.broadcast_to(mean, (16, width)).astype(BF16)
-        virtual[...] = dot(mean, wm[layer])
 
     def attend_in(layer, which, queries, at):
         count = count_sm[which]
@@ -371,11 +372,11 @@
             block,
         )
 
-    def early_copies(i):
-        at = pl.ds(i * group, group)
+    def early_copies(start, count):
+        at = pl.ds(start, count)
         return (
-            pltpu.make_async_copy(asked.at[at], queries_out.at[at], early_sem.at[0, i]),
-            pltpu.make_async_copy(arranged.at[at], latent_out.at[at], early_sem.at[1, i]),
+            pltpu.make_async_copy(asked.at[at], queries_out.at[at], early_sem.at[0]),
+            pltpu.make_async_copy(arranged.at[at], latent_out.at[at], early_sem.at[1]),
         )
 
     def block_step(layer, i):
@@ -402,7 +403,7 @@
         at = pl.ds(i * group, group)
         if last:
             early[at] = result.reshape(group, block, width)
-            for copy in early_copies(i):
+            for copy in early_copies(i * group, group):
                 copy.start()
         else:
             result = (result + virtual[0:1, :]).astype(BF16)
@@ -417,18 +418,21 @@
         return carry
 
     def drain(layer):
-        def one(k, carry):
-            to = lax.rem(me + k, peers)
-            far_out(layer, to).wait_send()
-            sum_out(layer, to).wait_send()
-            return carry
-
-        lax.fori_loop(1, peers, one, 0)
+        far_some(layer, 0, peers - 1, my_part).wait_send()
+        sum_all(layer).wait_send()
         halo_each(lambda side, to: halo_copy(layer, side, to).wait_send())
 
-    use(0, range(3))
+    settled = pltpu.make_async_copy(latent, settled_out, x_sem)
+
+    def settle(b, carry):
+        latent[b] = (early[b] + virtual[0:1, :]).astype(BF16)
+        return carry
+
+    for load in loads[:3]:
+        load.wait()
     gather(0)
-    use(0, range(3, count_w))
+    for load in loads[3:]:
+        load.wait()
     total_ref[0:1, :] = jnp.zeros((1, width), F32)
 
     def sending_step(i, carry):
@@ -472,56 +476,31 @@
     lax.fori_loop(blocks - HALO_B * middle, peers - 1, go_rest, 0)
     stage_self(1)
 
-    use(1, range(count_w))
     gather(1)
-    virtual_ref[...] = virtual[...]
-    settled = pltpu.make_async_copy(latent, settled_out, x_sem)
-
-    def settle(b, carry):
-        latent[b] = (early[b] + virtual[0:1, :]).astype(BF16)
-        return carry
-
-    lax.fori_loop(0, blocks, settle, 0)
-    settled.start()
     drain(1)
-
-    def await_own(n, carry):
-        for copy in export(HALO_B + n * chunk, chunk, n):
+    for start, count, n in ((HALO_B, blocks, 0), (near, peers * slots, 1)):
+        for copy in export(start, count, n):
             copy.wait()
-        return carry
-
-    def await_far(n, carry):
-        for copy in export(near + n * many * slots, many * slots, first_far + n):
-            copy.wait()
-        return carry
-
-    def await_early(n, carry):
-        for copy in early_copies(n):
-            copy.wait()
-        return carry
 
     @pl.when(me > 0)
     def _():
-        for copy in export(0, HALO_B, blocks // chunk):
+        for copy in export(0, HALO_B, 2):
             copy.wait()
 
     @pl.when(me < peers - 1)
     def _():
-        for copy in export(HALO_B + blocks, HALO_B, blocks // chunk + 1):
+        for copy in export(HALO_B + blocks, HALO_B, 3):
             copy.wait()
 
-    lax.fori_loop(0, blocks // chunk, await_own, 0)
-    lax.fori_loop(0, peers // many, await_far, 0)
-    lax.fori_loop(0, steps, await_early, 0)
+    for copy in early_copies(0, blocks):
+        copy.wait()
     settled.wait()
 
 
 def finish_kernel(layer, near, group, table_sm, count_sm, gains_ref, virtual_ref, settled_hbm, keys_hbm, values_hbm,
-                  queries_hbm, latent_hbm, wo_hbm, wu_hbm, wd_hbm, out_hbm, kept_keys, kept_values, asked, current, fresh,
-                  context, kept, wo, wu, wd, todo_sm, away_sm, w_sem, key_sem, value_sem, row_sem, out_sem,
-                  kept_sem, keep_sem):
-    blocks = table_sm.shape[0]
-    block, width = current.shape[1:]
+                  queries_hbm, latent_hbm, wo_hbm, wu_hbm, wd_hbm, out_hbm, kept_keys, kept_values, asked, current, context,
+                  kept, wo, wu, wd, todo_sm, w_sem, key_sem, value_sem, row_sem, kept_sem):
+    blocks, block, width = kept.shape
     listed = table_sm.shape[1]
     head = width // HEADS
     weight_loads = [
@@ -538,49 +517,45 @@
         def _(b=b, number=number):
             todo_sm[number] = b
 
-        away_sm[b] = away
         number = number + away
-
-    load_kept = pltpu.make_async_copy(settled_hbm, kept, kept_sem)
-
-    def keep(b, act):
-        @pl.when(away_sm[b] == 0)
-        def _():
-            act(pltpu.make_async_copy(kept.at[b], out_hbm.at[b], keep_sem.at[b]))
 
     def block_of(i, g):
         return todo_sm[jnp.minimum(i * group + g, number - 1)]
 
-    def fetch(i, g, act):
+    def rows(which, g):
+        return (
+            pltpu.make_async_copy(queries_hbm.at[which], asked.at[g], row_sem.at[0, g]),
+            pltpu.make_async_copy(latent_hbm.at[which], current.at[g], row_sem.at[1, g]),
+        )
+
+    def fetch(i, g):
         which = block_of(i, g)
-        act(pltpu.make_async_copy(queries_hbm.at[which], asked.at[g], row_sem.at[0, g]))
-        act(pltpu.make_async_copy(latent_hbm.at[which], current.at[g], row_sem.at[1, g]))
+        for copy in rows(which, g):
+            copy.start()
         for j in range(listed):
-            def one(j=j):
-                entry = table_sm[which, j]
-                act(pltpu.make_async_copy(keys_hbm.at[entry], kept_keys.at[g, j], key_sem.at[g, j]))
-                act(pltpu.make_async_copy(values_hbm.at[entry], kept_values.at[g, j], value_sem.at[g, j]))
-
-            if 2 * j < listed:
-                one()
-            else:
-                pl.when(j < count_sm[which])(one)
-
-    def begin(i):
+            entry = table_sm[which, j * below(j, count_sm[which])]
+            pltpu.make_async_copy(keys_hbm.at[entry], kept_keys.at[g, j], key_sem.at[g]).start()
+            pltpu.make_async_copy(values_hbm.at[entry], kept_values.at[g, j], value_sem.at[g]).start()
+
+    def fetched(i, g):
+        for copy in rows(block_of(i, g), g):
+            copy.wait()
+        some = pl.ds(0, listed)
+        pltpu.make_async_copy(keys_hbm.at[some], kept_keys.at[g], key_sem.at[g]).wait()
+        pltpu.make_async_copy(values_hbm.at[some], kept_values.at[g], value_sem.at[g]).wait()
+
+    def each_live(i, act):
         for g in range(group):
-            fetch(i, g, lambda copy: copy.start())
+            pl.when(i * group + g < number)(lambda g=g: act(i, g))
 
     def late_step(i, carry):
-        pl.when(i > 0)(lambda: begin(i))
+        pl.when(i > 0)(lambda: each_live(i, fetch))
+        each_live(i, fetched)
         for g in range(group):
-            which = block_of(i, g)
-            count = count_sm[which]
-            fetch(i, g, lambda copy: copy.wait())
-            spots = [j * below(j, count) for j in range(listed)]
             attend(
-                count,
-                lambda j, pair, g=g, spots=spots: kept_keys[g, spots[j], :, pair],
-                lambda j, pair, g=g, spots=spots: kept_values[g, spots[j], pair, :],
+                count_sm[block_of(i, g)],
+                lambda j, pair, g=g: kept_keys[g, j, :, pair],
+                lambda j, pair, g=g: kept_values[g, j, pair, :],
                 lambda part, g=g: asked[g, part, :],
                 context,
                 g * block,
@@ -591,42 +566,38 @@
 
         @pl.when(i == 0)
         def _():
-            load_kept.wait()
-            for b in range(blocks):
-                keep(b, lambda copy: copy.start())
             for load in weight_loads:
                 load.wait()
+            load_kept.wait()
 
         x = current[...].reshape(group * block, width).astype(F32)
         result = feed(x, context[...], wo[...], wu, wd, gains_ref, layer) + virtual_ref[0:1, :]
-        fresh[...] = result.astype(BF16).reshape(group, block, width)
-
-        def put(g):
-            return pltpu.make_async_copy(fresh.at[g], out_hbm.at[block_of(i, g)], out_sem.at[g])
-
-        for g in range(group):
-            pl.when(i * group + g < number)(lambda g=g: put(g).start())
-        for g in range(group):
-            pl.when(i * group + g < number)(lambda g=g: put(g).wait())
-        return carry
+        result = result.astype(BF16).reshape(group, block, width)
+
+        def put(i, g):
+            kept[block_of(i, g)] = result[g]
+
+        each_live(i, put)
+        return carry
+
+    load_kept = pltpu.make_async_copy(settled_hbm, kept, kept_sem)
 
     @pl.when(number > 0)
     def _():
-        begin(0)
-        load_kept.start()
+        each_live(0, fetch)
         for load in weight_loads:
             load.start()
+        load_kept.start()
         lax.fori_loop(0, (number + group - 1) // group, late_step, 0)
 
     @pl.when(number == 0)
     def _():
         load_kept.start()
         load_kept.wait()
-        for b in range(blocks):
-            keep(b, lambda copy: copy.start())
-
-    for b in range(blocks):
-        keep(b, lambda copy: copy.wait())
+
+    give = pltpu.make_async_copy(kept, out_hbm, kept_sem)
+    give.start()
+    give.wait()
 
 
 def body(node_features, nbr_table, nbr_count, send_block, w_query, w_key, w_value, w_out, w_up, w_down, w_virtual, gains):
@@ -644,8 +615,6 @@
     vmem, smem, hbm = (pl.BlockSpec(memory_space=s) for s in (pltpu.VMEM, pltpu.SMEM, pl.ANY))
     dma = pltpu.SemaphoreType.DMA
     shape = jax.ShapeDtypeStruct
-    steps = blocks // group
-    groups = blocks // math.gcd(blocks, 4) + 2 + peers // math.gcd(peers // 4, 4)
     scratch = [pltpu.VMEM(w.shape, BF16) for w in weights]
     scratch += [
         pltpu.VMEM((blocks, block, width), BF16),
@@ -665,18 +634,23 @@
         pltpu.VMEM((blocks, width, block), BF16),
         pltpu.VMEM((blocks, block, width), BF16),
         pltpu.VMEM((16, width), F32),
+        pltpu.SMEM(nbr_table.shape, jnp.int32),
+        pltpu.SMEM(nbr_count.shape, jnp.int32),
+        pltpu.SMEM((peers * slots,), jnp.int32),
+        pltpu.VMEM(gains.shape, F32),
         pltpu.SMEM((blocks,), jnp.int32),
         pltpu.SMEM((blocks,), jnp.int32),
         dma,
-        dma((layers, len(weights))),
-        dma((layers, peers)),
-        dma((layers, peers)),
+        dma((4,)),
+        dma((len(weights),)),
+        dma((layers,)),
+        dma((layers, 4)),
         dma((layers, 2)),
         dma((layers, 2)),
-        dma((layers, peers)),
-        dma((layers, peers)),
-        dma((2, groups)),
-        dma((2, steps)),
+        dma((layers,)),
+        dma((layers,)),
+        dma((2, 4)),
+        dma((2,)),
     ]
     settled, keys, values, queries, latent, virtual = pl.pallas_call(
         functools.partial(exchange_kernel, shapes),
@@ -688,7 +662,7 @@
             shape((blocks, block, width), BF16),
             shape((16, width), F32),
         ),
-        in_specs=[smem, smem, smem, vmem] + [hbm] * (1 + len(weights)),
+        in_specs=[hbm] * (5 + len(weights)),
         out_specs=(hbm, hbm, hbm, hbm, hbm, vmem),
         scratch_shapes=scratch,
         compiler_params=pltpu.CompilerParams(collective_id=0, has_side_effects=True, vmem_limit_bytes=VMEM_LIMIT),
@@ -704,21 +678,17 @@
             pltpu.VMEM((group, listed, width, block), BF16),
             pltpu.VMEM((group, width, block), BF16),
             pltpu.VMEM((group, block, width), BF16),
-            pltpu.VMEM((group, block, width), BF16),
             pltpu.VMEM((width, group * block), BF16),
             pltpu.VMEM((blocks, block, width), BF16),
             pltpu.VMEM(w_out.shape[1:], BF16),
             pltpu.VMEM(w_up.shape[1:], BF16),
             pltpu.VMEM(w_down.shape[1:], BF16),
             pltpu.SMEM((blocks,), jnp.int32),
-            pltpu.SMEM((blocks,), jnp.int32),
             dma((3,)),
-            dma((group, listed)),
-            dma((group, listed)),
+            dma((group,)),
+            dma((group,)),
             dma((2, group)),
-            dma((group,)),
             dma,
-            dma((blocks,)),
         ],
         compiler_params=pltpu.CompilerParams(vmem_limit_bytes=VMEM_LIMIT),
         name="finish",

time: 126 us -> 120 us (0.952)
  Pallas kernels: 125 us -> 119 us
    pallas_call x1, Pallas kernels: 110 us -> 107 us  [body(): pl.pallas_call(functools.partial(exchange_kernel, shapes), out_shape=(sha...]
    pallas_call x1, Pallas kernels: 14.2 us -> 11.3 us  [body(): pl.pallas_call(functools.partial(finish_kernel, layers - 1, near, group),...]
where the time goes in v4:
time: 120 us; the launch traced here: 119 us
  Pallas kernels  119 us (99%)
    pallas_call x1, Pallas kernels, body(): pl.pallas_call(functools.partial(exchange_kernel, shapes), out_shape=(sha...  107 us
    pallas_call x1, Pallas kernels, body(): pl.pallas_call(functools.partial(finish_kernel, layers - 1, near, group),...  11.3 us

profile of v4, /device:TPU:0, one launch (start us, length us, event | category | flops | bytes accessed | tf_op | source)
XLA Modules:
  0.0 118.8 jit_solution(10222269851949060965)
XLA Ops:
  0.0 107.3 %exchange.1 = (bf16[8,128,512]{2,1,0:T(8,128)(2,1)}, bf16[28,128,512]{2,1,0:T(8,128)(2,1)}, bf16[28,512,128]{2,1,0:T(8,128)(2,1)}, bf16[8,512,128]{2,1,0:T(8,128...) custom-call(s32[8,8]{1,0:T(8,128)} %table_sm.1, s32[8]{0:T(128)} %count_sm.1, s32[16]{0:T(128)} %bitcast.4, ...), custom_call_target="tpu_custom_call" | custom-call | tf_op jit(solution)/shard_map/exchange/pallas_call | solution.py:655
  107.4 11.3 %finish.1 = bf16[8,128,512]{2,1,0:T(8,128)(2,1)} custom-call(s32[8,8]{1,0:T(8,128)} %table_sm.1, s32[8]{0:T(128)} %count_sm.1, f32[2,4,512]{2,1,0:T(4,128)} %gains_ref.1, f32[16,512]{1,0:T(8,128)} %get-tuple-element.11.virtual_ref, bf16[8,128,512]{2,1,0:T(8,128)(2,1)} %get-tuple-element.12.settled_hbm, bf16[28,128,512]{2,1,0:T(8,128)(2,1)} %get-tuple-element.13.keys_hbm, ...), custom_call_target="tpu_custom_call" | custom-call | tf_op jit(solution)/shard_map/finish/pallas_call | solution.py:671

commit v5 on v4

--- a/solution.py
+++ b/solution.py
@@ -212,7 +212,6 @@
             halo_send[layer, side, pl.ds(b * block, block), :] = normed[layer, at]
 
     def send_halo(layer, across=None):
-        halo_each(lambda side, to: stage_halo(layer, side), across)
         halo_each(lambda side, to: halo_copy(layer, side, to).start(), across)
 
     def stage_sum(layer):
@@ -237,6 +236,7 @@
         return carry
 
     stage_sum(0)
+    halo_each(lambda side, to: stage_halo(0, side))
     lax.fori_loop(0, peers - 1, stage_all, 0)
     pl.semaphore_wait(barrier, peers - 1)
     send_halo(0)
@@ -440,13 +440,12 @@
 
         @pl.when(i == 0)
         def _():
-            send_halo(1, 1)
+            halo_each(lambda side, to: stage_halo(1, side), 1)
 
         @pl.when(i == steps - 1)
         def _():
+            halo_each(lambda side, to: stage_halo(1, side), 0)
             stage_sum(1)
-            send_halo(1, 0)
-            send_sum(1)
 
         held = HALO_B * middle
         begin = jnp.maximum(i * group - held, 0)
@@ -459,21 +458,22 @@
             far_out(1, order(1, k)).start()
             return carry
 
-        lax.fori_loop(begin, end, each, 0)
-        lax.fori_loop(begin, end, go, 0)
-        return carry
-
-    def rest(k, carry):
-        stage(1, order(1, k))
-        return carry
-
-    def go_rest(k, carry):
-        far_out(1, order(1, k)).start()
+        until = jnp.where(i == steps - 1, peers - 1, end)
+        lax.fori_loop(begin, until, each, 0)
+
+        @pl.when(i == 0)
+        def _():
+            send_halo(1, 1)
+
+        @pl.when(i == steps - 1)
+        def _():
+            send_halo(1, 0)
+            send_sum(1)
+
+        lax.fori_loop(begin, until, go, 0)
         return carry
 
     lax.fori_loop(0, steps, sending_step, 0)
-    lax.fori_loop(blocks - HALO_B * middle, peers - 1, rest, 0)
-    lax.fori_loop(blocks - HALO_B * middle, peers - 1, go_rest, 0)
     stage_self(1)
 
     gather(1)
@@ -519,76 +519,92 @@
 
         number = number + away
 
-    def block_of(i, g):
-        return todo_sm[jnp.minimum(i * group + g, number - 1)]
-
-    def rows(which, g):
+    def block_of(n):
+        return todo_sm[jnp.minimum(n, number - 1)]
+
+    def rows(n):
+        which = block_of(n)
         return (
-            pltpu.make_async_copy(queries_hbm.at[which], asked.at[g], row_sem.at[0, g]),
-            pltpu.make_async_copy(latent_hbm.at[which], current.at[g], row_sem.at[1, g]),
-        )
-
-    def fetch(i, g):
-        which = block_of(i, g)
-        for copy in rows(which, g):
+            pltpu.make_async_copy(queries_hbm.at[which], asked.at[n], row_sem.at[0, n]),
+            pltpu.make_async_copy(latent_hbm.at[which], current.at[n], row_sem.at[1, n]),
+        )
+
+    def fetch(n, carry):
+        which = block_of(n)
+        for copy in rows(n):
             copy.start()
         for j in range(listed):
             entry = table_sm[which, j * below(j, count_sm[which])]
-            pltpu.make_async_copy(keys_hbm.at[entry], kept_keys.at[g, j], key_sem.at[g]).start()
-            pltpu.make_async_copy(values_hbm.at[entry], kept_values.at[g, j], value_sem.at[g]).start()
-
-    def fetched(i, g):
-        for copy in rows(block_of(i, g), g):
+            pltpu.make_async_copy(keys_hbm.at[entry], kept_keys.at[n, j], key_sem.at[n]).start()
+            pltpu.make_async_copy(values_hbm.at[entry], kept_values.at[n, j], value_sem.at[n]).start()
+        return carry
+
+    def fetched(n):
+        for copy in rows(n):
             copy.wait()
         some = pl.ds(0, listed)
-        pltpu.make_async_copy(keys_hbm.at[some], kept_keys.at[g], key_sem.at[g]).wait()
-        pltpu.make_async_copy(values_hbm.at[some], kept_values.at[g], value_sem.at[g]).wait()
-
-    def each_live(i, act):
-        for g in range(group):
-            pl.when(i * group + g < number)(lambda g=g: act(i, g))
-
-    def late_step(i, carry):
-        pl.when(i > 0)(lambda: each_live(i, fetch))
-        each_live(i, fetched)
-        for g in range(group):
+        pltpu.make_async_copy(keys_hbm.at[some], kept_keys.at[n], key_sem.at[n]).wait()
+        pltpu.make_async_copy(values_hbm.at[some], kept_values.at[n], value_sem.at[n]).wait()
+
+    load_kept = pltpu.make_async_copy(settled_hbm, kept, kept_sem)
+    together = context.shape[2] // block
+    turns = (number + together - 1) // together
+
+    def attend_some(i, carry):
+        for g in range(together):
+            pl.when(i * together + g < number)(lambda g=g: fetched(i * together + g))
+
+        @pl.when(i == 0)
+        def _():
+            for load in weight_loads:
+                load.start()
+            load_kept.start()
+
+        for g in range(together):
+            n = i * together + g
             attend(
-                count_sm[block_of(i, g)],
-                lambda j, pair, g=g: kept_keys[g, j, :, pair],
-                lambda j, pair, g=g: kept_values[g, j, pair, :],
-                lambda part, g=g: asked[g, part, :],
-                context,
+                count_sm[block_of(n)],
+                lambda j, pair, n=n: kept_keys[n, j, :, pair],
+                lambda j, pair, n=n: kept_values[n, j, pair, :],
+                lambda part, n=n: asked[n, part, :],
+                context.at[i],
                 g * block,
                 listed,
                 head,
                 block,
             )
-
-        @pl.when(i == 0)
-        def _():
-            for load in weight_loads:
-                load.wait()
-            load_kept.wait()
-
-        x = current[...].reshape(group * block, width).astype(F32)
-        result = feed(x, context[...], wo[...], wu, wd, gains_ref, layer) + virtual_ref[0:1, :]
-        result = result.astype(BF16).reshape(group, block, width)
-
-        def put(i, g):
-            kept[block_of(i, g)] = result[g]
-
-        each_live(i, put)
-        return carry
-
-    load_kept = pltpu.make_async_copy(settled_hbm, kept, kept_sem)
+        return carry
+
+    def feed_some(i, parts):
+        size = parts * together
+        first = i * group
+        x = current[pl.ds(first, size)].reshape(size * block, width).astype(F32)
+        mixed = jnp.concatenate([context[i * (group // together) + n] for n in range(parts)], axis=1)
+        result = feed(x, mixed, wo[...], wu, wd, gains_ref, layer) + virtual_ref[0:1, :]
+        result = result.astype(BF16).reshape(size, block, width)
+        for g in range(size):
+
+            @pl.when(first + g < number)
+            def _(g=g):
+                kept[block_of(first + g)] = result[g]
+
+    def feed_turns(i, carry):
+        left = number - i * group
+        if group > together:
+            pl.when(left > together)(lambda: feed_some(i, group // together))
+            pl.when(left <= together)(lambda: feed_some(i, 1))
+        else:
+            feed_some(i, 1)
+        return carry
 
     @pl.when(number > 0)
     def _():
-        each_live(0, fetch)
+        lax.fori_loop(0, number, fetch, 0)
+        lax.fori_loop(0, turns, attend_some, 0)
         for load in weight_loads:
-            load.start()
-        load_kept.start()
-        lax.fori_loop(0, (number + group - 1) // group, late_step, 0)
+            load.wait()
+        load_kept.wait()
+        lax.fori_loop(0, (number + group - 1) // group, feed_turns, 0)
 
     @pl.when(number == 0)
     def _():
@@ -674,20 +690,20 @@
         in_specs=[smem, smem, vmem, vmem] + [hbm] * 8,
         out_specs=hbm,
         scratch_shapes=[
-            pltpu.VMEM((group, listed, block, width), BF16),
-            pltpu.VMEM((group, listed, width, block), BF16),
-            pltpu.VMEM((group, width, block), BF16),
-            pltpu.VMEM((group, block, width), BF16),
-            pltpu.VMEM((width, group * block), BF16),
+            pltpu.VMEM((blocks, listed, block, width), BF16),
+            pltpu.VMEM((blocks, listed, width, block), BF16),
+            pltpu.VMEM((blocks, width, block), BF16),
+            pltpu.VMEM((blocks, block, width), BF16),
+            pltpu.VMEM((blocks // math.gcd(group, 2), width, math.gcd(group, 2) * block), BF16),
             pltpu.VMEM((blocks, block, width), BF16),
             pltpu.VMEM(w_out.shape[1:], BF16),
             pltpu.VMEM(w_up.shape[1:], BF16),
             pltpu.VMEM(w_down.shape[1:], BF16),
             pltpu.SMEM((blocks,), jnp.int32),
             dma((3,)),
-            dma((group,)),
-            dma((group,)),
-            dma((2, group)),
+            dma((blocks,)),
+            dma((blocks,)),
+            dma((2, blocks)),
             dma,
         ],
         compiler_params=pltpu.CompilerParams(vmem_limit_bytes=VMEM_LIMIT),

time: 120 us -> 119 us (level); the launches traced: 119 us -> 119 us
  no operation moved by 1% of the time
where the time goes in v5:
time: 119 us
  Pallas kernels  119 us (100%)
    pallas_call x1, Pallas kernels, body(): pl.pallas_call(functools.partial(exchange_kernel, shapes), out_shape=(sha...  107 us
    pallas_call x1, Pallas kernels, body(): pl.pallas_call(functools.partial(finish_kernel, layers - 1, near, group),...  11.8 us

profile of v5, /device:TPU:0, one launch (start us, length us, event | category | flops | bytes accessed | tf_op | source)
XLA Modules:
  0.0 119.2 jit_solution(14306782173898374849)
XLA Ops:
  0.0 107.2 %exchange.1 = (bf16[8,128,512]{2,1,0:T(8,128)(2,1)}, bf16[28,128,512]{2,1,0:T(8,128)(2,1)}, bf16[28,512,128]{2,1,0:T(8,128)(2,1)}, bf16[8,512,128]{2,1,0:T(8,128...) custom-call(s32[8,8]{1,0:T(8,128)} %table_sm.1, s32[8]{0:T(128)} %count_sm.1, s32[16]{0:T(128)} %bitcast.4, ...), custom_call_target="tpu_custom_call" | custom-call | tf_op jit(solution)/shard_map/exchange/pallas_call | solution.py:671
  107.2 11.8 %finish.1 = bf16[8,128,512]{2,1,0:T(8,128)(2,1)} custom-call(s32[8,8]{1,0:T(8,128)} %table_sm.1, s32[8]{0:T(128)} %count_sm.1, f32[2,4,512]{2,1,0:T(4,128)} %gains_ref.1, f32[16,512]{1,0:T(8,128)} %get-tuple-element.11.virtual_ref, bf16[8,128,512]{2,1,0:T(8,128)(2,1)} %get-tuple-element.12.settled_hbm, bf16[28,128,512]{2,1,0:T(8,128)(2,1)} %get-tuple-element.13.keys_hbm, ...), custom_call_target="tpu_custom_call" | custom-call | tf_op jit(solution)/shard_map/finish/pallas_call | solution.py:687

commit v6 on v5

--- a/solution.py
+++ b/solution.py
@@ -554,6 +554,8 @@
         for g in range(together):
             pl.when(i * together + g < number)(lambda g=g: fetched(i * together + g))
 
+        lax.fori_loop((i + 1) * together, jnp.minimum((i + 2) * together, number), fetch, 0)
+
         @pl.when(i == 0)
         def _():
             for load in weight_loads:
@@ -599,7 +601,7 @@
 
     @pl.when(number > 0)
     def _():
-        lax.fori_loop(0, number, fetch, 0)
+        lax.fori_loop(0, jnp.minimum(together, number), fetch, 0)
         lax.fori_loop(0, turns, attend_some, 0)
         for load in weight_loads:
             load.wait()

time: 119 us -> 121 us (1.017)
  Pallas kernels: 119 us -> 121 us
    pallas_call x1, Pallas kernels: 11.8 us -> 13.4 us  [body(): pl.pallas_call(functools.partial(finish_kernel, layers - 1, near, group),...]
where the time goes in v6:
time: 121 us
  Pallas kernels  121 us (100%)
    pallas_call x1, Pallas kernels, body(): pl.pallas_call(functools.partial(exchange_kernel, shapes), out_shape=(sha...  107 us
    pallas_call x1, Pallas kernels, body(): pl.pallas_call(functools.partial(finish_kernel, layers - 1, near, group),...  13.4 us

profile of v6, /device:TPU:0, one launch (start us, length us, event | category | flops | bytes accessed | tf_op | source)
XLA Modules:
  0.0 120.8 jit_solution(11608762683891154477)
XLA Ops:
  0.0 107.2 %exchange.1 = (bf16[8,128,512]{2,1,0:T(8,128)(2,1)}, bf16[28,128,512]{2,1,0:T(8,128)(2,1)}, bf16[28,512,128]{2,1,0:T(8,128)(2,1)}, bf16[8,512,128]{2,1,0:T(8,128...) custom-call(s32[8,8]{1,0:T(8,128)} %table_sm.1, s32[8]{0:T(128)} %count_sm.1, s32[16]{0:T(128)} %bitcast.4, ...), custom_call_target="tpu_custom_call" | custom-call | tf_op jit(solution)/shard_map/exchange/pallas_call | solution.py:673
  107.2 13.4 %finish.1 = bf16[8,128,512]{2,1,0:T(8,128)(2,1)} custom-call(s32[8,8]{1,0:T(8,128)} %table_sm.1, s32[8]{0:T(128)} %count_sm.1, f32[2,4,512]{2,1,0:T(4,128)} %gains_ref.1, f32[16,512]{1,0:T(8,128)} %get-tuple-element.11.virtual_ref, bf16[8,128,512]{2,1,0:T(8,128)(2,1)} %get-tuple-element.12.settled_hbm, bf16[28,128,512]{2,1,0:T(8,128)(2,1)} %get-tuple-element.13.keys_hbm, ...), custom_call_target="tpu_custom_call" | custom-call | tf_op jit(solution)/shard_map/finish/pallas_call | solution.py:689

commit v7 on v6

--- a/solution.py
+++ b/solution.py
@@ -86,6 +86,21 @@
         term = dot(hidden, wd[f : f + part, :])
         down = term if down is None else down + term
     return after_att + normalize(down, gains_ref[layer, 3:4, :])
+
+
+class Parts:
+    def __init__(self, src, dst, sem, parts):
+        self.whole = pltpu.make_async_copy(src, dst, sem)
+        size = dst.shape[0] // math.gcd(dst.shape[0], parts)
+        slices = [pl.ds(start, size) for start in range(0, dst.shape[0], size)]
+        self.pieces = [pltpu.make_async_copy(src.at[part], dst.at[part], sem) for part in slices]
+
+    def start(self):
+        for piece in self.pieces:
+            piece.start()
+
+    def wait(self):
+        self.whole.wait()
 
 
 def exchange_kernel(shapes, table_hbm, count_hbm, send_hbm, gains_hbm, x_hbm, wq_hbm, wk_hbm, wv_hbm, wo_hbm, wu_hbm,
@@ -152,7 +167,7 @@
             def _(side=side):
                 act(side, me - 1 if side == 0 else me + 1)
 
-    load_x = pltpu.make_async_copy(x_hbm, x_ref, x_sem)
+    load_x = Parts(x_hbm, x_ref, x_sem, 8)
     load_x.start()
     smalls = [
         pltpu.make_async_copy(src, dst, small_sem.at[n])
@@ -504,8 +519,8 @@
     listed = table_sm.shape[1]
     head = width // HEADS
     weight_loads = [
-        pltpu.make_async_copy(src.at[layer], dst, w_sem.at[n])
-        for n, (src, dst) in enumerate(((wo_hbm, wo), (wu_hbm, wu), (wd_hbm, wd)))
+        Parts(src.at[layer], dst, w_sem.at[n], parts)
+        for n, (src, dst, parts) in enumerate(((wo_hbm, wo, 4), (wu_hbm, wu, 16), (wd_hbm, wd, 16)))
     ]
     number = jnp.int32(0)
     for b in range(blocks):
@@ -546,7 +561,7 @@
         pltpu.make_async_copy(keys_hbm.at[some], kept_keys.at[n], key_sem.at[n]).wait()
         pltpu.make_async_copy(values_hbm.at[some], kept_values.at[n], value_sem.at[n]).wait()
 
-    load_kept = pltpu.make_async_copy(settled_hbm, kept, kept_sem)
+    load_kept = Parts(settled_hbm, kept, kept_sem, 8)
     together = context.shape[2] // block
     turns = (number + together - 1) // together
 
@@ -613,7 +628,7 @@
         load_kept.start()
         load_kept.wait()
 
-    give = pltpu.make_async_copy(kept, out_hbm, kept_sem)
+    give = Parts(kept, out_hbm, kept_sem, 8)
     give.start()
     give.wait()
 

time: 121 us -> 119 us (0.983); the launches traced: 121 us -> 117 us
  Pallas kernels: 121 us -> 117 us
    pallas_call x1, Pallas kernels: 13.4 us -> 9.85 us  [body(): pl.pallas_call(functools.partial(finish_kernel, layers - 1, near, group),...]
where the time goes in v7:
time: 119 us; the launch traced here: 117 us
  Pallas kernels  117 us (98%)
    pallas_call x1, Pallas kernels, body(): pl.pallas_call(functools.partial(exchange_kernel, shapes), out_shape=(sha...  107 us
    pallas_call x1, Pallas kernels, body(): pl.pallas_call(functools.partial(finish_kernel, layers - 1, near, group),...  9.85 us

profile of v7, /device:TPU:0, one launch (start us, length us, event | category | flops | bytes accessed | tf_op | source)
XLA Modules:
  0.0 117.3 jit_solution(17994339320762971139)
XLA Ops:
  0.0 107.3 %exchange.1 = (bf16[8,128,512]{2,1,0:T(8,128)(2,1)}, bf16[28,128,512]{2,1,0:T(8,128)(2,1)}, bf16[28,512,128]{2,1,0:T(8,128)(2,1)}, bf16[8,512,128]{2,1,0:T(8,128...) custom-call(s32[8,8]{1,0:T(8,128)} %table_sm.1, s32[8]{0:T(128)} %count_sm.1, s32[16]{0:T(128)} %bitcast.4, ...), custom_call_target="tpu_custom_call" | custom-call | tf_op jit(solution)/shard_map/exchange/pallas_call | solution.py:688
  107.3 9.8 %finish.1 = bf16[8,128,512]{2,1,0:T(8,128)(2,1)} custom-call(s32[8,8]{1,0:T(8,128)} %table_sm.1, s32[8]{0:T(128)} %count_sm.1, f32[2,4,512]{2,1,0:T(4,128)} %gains_ref.1, f32[16,512]{1,0:T(8,128)} %get-tuple-element.11.virtual_ref, bf16[8,128,512]{2,1,0:T(8,128)(2,1)} %get-tuple-element.12.settled_hbm, bf16[28,128,512]{2,1,0:T(8,128)(2,1)} %get-tuple-element.13.keys_hbm, ...), custom_call_target="tpu_custom_call" | custom-call | tf_op jit(solution)/shard_map/finish/pallas_call | solution.py:704

commit v8 on v7

--- a/solution.py
+++ b/solution.py
@@ -571,7 +571,7 @@
 
         lax.fori_loop((i + 1) * together, jnp.minimum((i + 2) * together, number), fetch, 0)
 
-        @pl.when(i == 0)
+        @pl.when(i == jnp.minimum(1, turns - 1))
         def _():
             for load in weight_loads:
                 load.start()

time: 119 us -> 119 us (level)
  no operation moved by 1% of the time
where the time goes in v8:
time: 119 us; the launch traced here: 117 us
  Pallas kernels  116 us (97%)
    pallas_call x1, Pallas kernels, body(): pl.pallas_call(functools.partial(exchange_kernel, shapes), out_shape=(sha...  107 us
    pallas_call x1, Pallas kernels, body(): pl.pallas_call(functools.partial(finish_kernel, layers - 1, near, group),...  9.11 us

profile of v8, /device:TPU:0, one launch (start us, length us, event | category | flops | bytes accessed | tf_op | source)
XLA Modules:
  0.0 116.6 jit_solution(265027843963992441)
XLA Ops:
  0.0 107.3 %exchange.1 = (bf16[8,128,512]{2,1,0:T(8,128)(2,1)}, bf16[28,128,512]{2,1,0:T(8,128)(2,1)}, bf16[28,512,128]{2,1,0:T(8,128)(2,1)}, bf16[8,512,128]{2,1,0:T(8,128...) custom-call(s32[8,8]{1,0:T(8,128)} %table_sm.1, s32[8]{0:T(128)} %count_sm.1, s32[16]{0:T(128)} %bitcast.4, ...), custom_call_target="tpu_custom_call" | custom-call | tf_op jit(solution)/shard_map/exchange/pallas_call | solution.py:688
  107.3 9.1 %finish.1 = bf16[8,128,512]{2,1,0:T(8,128)(2,1)} custom-call(s32[8,8]{1,0:T(8,128)} %table_sm.1, s32[8]{0:T(128)} %count_sm.1, f32[2,4,512]{2,1,0:T(4,128)} %gains_ref.1, f32[16,512]{1,0:T(8,128)} %get-tuple-element.11.virtual_ref, bf16[8,128,512]{2,1,0:T(8,128)(2,1)} %get-tuple-element.12.settled_hbm, bf16[28,128,512]{2,1,0:T(8,128)(2,1)} %get-tuple-element.13.keys_hbm, ...), custom_call_target="tpu_custom_call" | custom-call | tf_op jit(solution)/shard_map/finish/pallas_call | solution.py:704
